TPU v7x, 32 devices: a whole 2x2x4 slice. The times are simulated.
32 devices in a mesh: layer: 4 (over y, core), row: 8 (over z, x).
Axes of the slice: x: 2, y: 2, z: 4, core: 2. Of those that a mesh axis runs over, the one named last changes fastest.
Arguments:
- rhs_leaf: float32 [8192, 128], P(('layer', 'row')), may hold values from -6 to 6
- rhs_anc: float32 [1024, 128], P('row'), may hold values from -6 to 6
- leaf_inv: float32 [64, 128, 128], P(('layer', 'row')), may hold values from -0.4 to 1.4, as said below
- leaf_low: float32 [32, 128, 128], P(('layer', 'row')), may hold values from -0.5 to 0.5
- couple: float32 [4096, 128, 128], P(('layer', 'row')), may hold values from -0.0234375 to 0.0234375
- tile_cols: int32 [32, 128], P(('layer', 'row')), may hold values from 0 to 15
- anc_inv: float32 [8, 128, 128], P('row'), may hold values from -0.4 to 1.4, as said below
- anc_low: float32 [8, 128, 128], P('row'), may hold values from -0.4375 to 0.4375
Outputs:
- leaf_solution: float32 [8192, 128], P(('layer', 'row'))
- anc_solution: float32 [1024, 128], P('row')
Inputs may be any that keep to these rules, and one draw needn't show every extreme that they name: `leaf_inv`: entries of an inverse tile: the identity plus noise of at most 0.4 in size on every entry. `anc_inv`: entries of an inverse tile: the identity plus noise of at most 0.4 in size on every entry. `tile_cols`: A tile index into the leaf rows of the block's own layer; repeats allowed.
All inputs are finite; a program needn't handle non-finite values.
Results may differ from a plain program's by a relative error of at most 0.0002.
Values sent between devices are 32-bit elements; how exact they have to be, the bound alone decides.
No kernel may reach another device: no remote copies, remote signals or barrier semaphores. Data moves between devices by JAX's collectives and lax.ppermute only.
A program may use at most 64 MiB of HBM per device.

v0:
```python
import functools
import math

import jax
import jax.numpy as jnp
from jax import lax
from jax.experimental import pallas as pl
from jax.experimental.pallas import tpu as pltpu
from jax.sharding import PartitionSpec as P


F32 = jnp.float32
VM = pl.BlockSpec(memory_space=pltpu.VMEM)
SM = pl.BlockSpec(memory_space=pltpu.SMEM)


def split(value, axis):
    high = value.astype(jnp.bfloat16)
    low = (value - high.astype(F32)).astype(jnp.bfloat16)
    return jnp.concatenate([high, low], axis=axis)


def spread(left, wide):
    rows, width = left.shape[0], wide.shape[1] // 2
    out = jnp.dot(split(left, 0), wide, preferred_element_type=F32)
    cross = out[:rows, width:] + out[rows:, :width]
    return out[:rows, :width] + (cross + out[rows:, width:])


def dot(left, right):
    return spread(left, split(right, 1))


def shape(*dims, dtype=F32):
    return jax.ShapeDtypeStruct(dims, dtype)


def room(scratch, outs=()):
    arrays = [v for v in [*scratch, *outs] if v.dtype in (F32, jnp.bfloat16)]
    size = sum(math.prod(v.shape) * jnp.dtype(v.dtype).itemsize for v in arrays)
    return pltpu.CompilerParams(vmem_limit_bytes=2 * size + (6 << 20))


def call(body, outs, far=(), arrived=(), scratch=(), stay=False):
    arrived = [pltpu.with_memory_space_constraint(v, pltpu.VMEM) for v in arrived]
    if stay:
        outs = [pltpu.VMEM(o.shape, o.dtype) for o in outs]
    copies = [pltpu.VMEM(v.shape, v.dtype) for v in far]
    if far:
        copies.append(pltpu.SemaphoreType.DMA((len(far),)))
    scratch = copies + list(scratch)
    return pl.pallas_call(
        body, out_shape=list(outs), compiler_params=room(scratch, outs),
        in_specs=[pl.BlockSpec(memory_space=pl.ANY)] * len(far) + [VM] * len(arrived),
        out_specs=[VM] * len(outs), scratch_shapes=scratch,
    )(*far, *arrived)


def fetch(sources, copies):
    started = [
        pltpu.make_async_copy(source, target, copies[len(sources)].at[i])
        for i, (source, target) in enumerate(zip(sources, copies))
    ]
    for copy in started:
        copy.start()

    def ready(i):
        started[i].wait()
        return copies[i]

    return ready


def pair_swap(value, axis, distance):
    count = lax.axis_size(axis)
    return lax.ppermute(value, axis, [(i, i ^ distance) for i in range(count)])


def leaf_body(*refs):
    ready = fetch(refs[:5], refs[7:])
    msg, anc = refs[5:7]
    tile = msg.shape[1]
    tiles = msg.shape[0] // tile
    half = tile // 2
    core = lax.axis_index("layer") % 2
    rhs, inv, low = ready(0), ready(1), ready(2)
    above = None
    for t in range(tiles):
        source = rhs[t * tile:(t + 1) * tile, :]
        if t > 0:
            source = source - dot(low[t - 1], above)
        above = dot(inv[t], source)
        msg[t * tile:(t + 1) * tile, :] = above
    start = pl.multiple_of(core * half, half)
    anc[:half, :] = ready(3)[0, pl.ds(start, half), :]
    anc[half:, :] = ready(4)[0, pl.ds(start, half), :]


def merge_body(leaf_tiles, chunk, cols, couple, *rest):
    place = lax.axis_index("row")
    outs, (buf, acc_a, acc_b, sems) = rest[:-4], rest[-4:]
    parts = couple.shape[0] // chunk
    started = [
        pltpu.make_async_copy(
            couple.at[pl.ds(i * chunk, chunk)], buf.at[pl.ds(i * chunk, chunk)], sems.at[i])
        for i in range(parts)
    ]
    for copy in started:
        copy.start()
    acc_a[...] = jnp.zeros_like(acc_a)
    acc_b[...] = jnp.zeros_like(acc_b)

    def add(acc, k):
        col = cols[0, k]
        owner = lax.div(col, leaf_tiles)
        acc[(owner ^ place) * leaf_tiles + col - owner * leaf_tiles] += buf[k]

    for i in range(parts):
        started[i].wait()

        def one(j, carry):
            add(acc_a, i * chunk + 2 * j)
            add(acc_b, i * chunk + 2 * j + 1)
            return carry

        lax.fori_loop(0, chunk // 2, one, 0, unroll=4)
    for i, out in enumerate(outs):
        for t in range(leaf_tiles):
            out[t] = acc_a[i * leaf_tiles + t] + acc_b[i * leaf_tiles + t]


def merge(couple, cols, leaf_tiles):
    k_all, tile, _ = couple.shape
    rows = lax.axis_size("row")
    chunk = 16 if k_all % 16 == 0 else k_all
    acc = pltpu.VMEM((rows * leaf_tiles, tile, tile), F32)
    scratch = [pltpu.VMEM(couple.shape, F32), acc, acc]
    return pl.pallas_call(
        functools.partial(merge_body, leaf_tiles, chunk), name="merge",
        in_specs=[SM, pl.BlockSpec(memory_space=pl.ANY)],
        out_specs=[VM] * rows, out_shape=[pltpu.VMEM((leaf_tiles, tile, tile), F32)] * rows,
        compiler_params=room(scratch),
        scratch_shapes=scratch + [pltpu.SemaphoreType.DMA((k_all // chunk,))],
    )(cols, couple)


def partial_body(count, *refs):
    ready = fetch(refs[:2], refs[2 * count + 4:])
    mats, msgs = refs[2:2 + count], refs[2 + count:1 + 2 * count]
    own, other, right = refs[1 + 2 * count:4 + 2 * count]
    buf = refs[-1]
    leaf_tiles, tile, _ = mats[0].shape
    half = tile // 2
    core = lax.axis_index("layer") % 2
    wide, thin = None, None
    for i in list(range(1, count)) + [0]:
        msg = msgs[i - 1] if i else ready(0)
        right_side = split(msg[...], 1)
        row = jnp.concatenate([mats[i][t] for t in range(leaf_tiles)], axis=1)
        high = row.astype(jnp.bfloat16)
        low = (row - high.astype(F32)).astype(jnp.bfloat16)
        a = jnp.dot(high, right_side, preferred_element_type=F32)
        b = jnp.dot(low, right_side[:, :right_side.shape[1] // 2], preferred_element_type=F32)
        wide = a if wide is None else wide + a
        thin = b if thin is None else thin + b
    cols = thin.shape[1]
    total = wide[:, :cols] + (wide[:, cols:] + thin)
    up = pl.multiple_of(core * half, half)
    down = pl.multiple_of((1 - core) * half, half)
    buf[...] = total.T
    own[...] = buf[pl.ds(up, half), :]
    other[...] = buf[pl.ds(down, half), :]
    buf[...] = ready(1)[...].T
    right[...] = buf[pl.ds(up, half), :]


def stack_body(*refs):
    ready = fetch(refs[:1], refs[-2:])
    out = refs[-3]
    for i in range(1, len(refs) - 3):
        out[i] = refs[i][...]
    out[0] = ready(0)[...]


def solve_body(count, *refs):
    mine, theirs = refs[:2]
    pieces = refs[2:2 + count]
    z, buf, a_buf, l_buf = refs[2 + count:]
    tile = a_buf.shape[1]
    half = tile // 2
    core = lax.axis_index("layer") % 2
    place = lax.axis_index("row")
    up = pl.multiple_of(core * half, half)
    down = pl.multiple_of((1 - core) * half, half)
    for i in range(count):
        r = place ^ i
        a_buf[r, pl.ds(up, half), :] = mine[i, :half, :]
        a_buf[r, pl.ds(down, half), :] = theirs[i, :half, :]
        l_buf[r, pl.ds(up, half), :] = mine[i, half:, :]
        l_buf[r, pl.ds(down, half), :] = theirs[i, half:, :]
        buf[r] = pieces[i][...]
    a = [split(a_buf[r], 1) for r in range(count)]
    y = []
    for r in range(count):
        value = spread(buf[r], split(a_buf[r].T, 1))
        if r > 0:
            value = value - dot(y[-1], spread(a_buf[r], split(l_buf[r], 1)).T)
        y.append(value)
    behind = None
    for r in range(count - 1, -1, -1):
        value = spread(y[r], a[r])
        if behind is not None:
            value = value - dot(behind, spread(l_buf[r + 1], a[r]))
        behind = value
        z[r] = behind


def final_body(count, *refs):
    ready = fetch(refs[:4], refs[7 + count:])
    z_mine, z_theirs = refs[4:6]
    mats = refs[6:5 + count]
    leaf, anc = refs[5 + count:7 + count]
    zt = refs[-1]
    leaf_tiles, tile, _ = refs[0].shape
    half = tile // 2
    core = lax.axis_index("layer") % 2
    place = lax.axis_index("row")
    zt[:, pl.ds(pl.multiple_of(core * half, half), half), :] = z_mine[...]
    zt[:, pl.ds(pl.multiple_of((1 - core) * half, half), half), :] = z_theirs[...]
    anc[...] = zt[place].T
    cols = zt.shape[1]
    both, single = None, None
    for i in list(range(1, count)) + [0]:
        mat = mats[i - 1] if i else ready(0)
        left = split(zt[place ^ i], 0)
        row = jnp.concatenate([mat[t] for t in range(leaf_tiles)], axis=1)
        high = row.astype(jnp.bfloat16)
        low_part = (row - high.astype(F32)).astype(jnp.bfloat16)
        p = jnp.dot(left, high, preferred_element_type=F32)
        q = jnp.dot(left[:cols], low_part, preferred_element_type=F32)
        both = p if both is None else both + p
        single = q if single is None else single + q
    total = both[:cols] + (both[cols:] + single)
    x, inv, low = ready(1), ready(2), ready(3)
    below = None
    for t in range(leaf_tiles - 1, -1, -1):
        rows = slice(t * tile, (t + 1) * tile)
        source = x[rows, :].T - total[:, rows]
        if below is not None:
            source = source - dot(below, low[t])
        below = dot(source, inv[t])
        leaf[rows, :] = below.T


def gather_row(msg, far):
    out = [msg, None] + [None] * (2 * far - 2)
    for k in range(far - 1, 0, -1):
        out[2 * k] = pair_swap(msg, "row", 2 * k)
    for k in range(far):
        out[2 * k + 1] = pair_swap(out[2 * k], "row", 1)
    return out


def per_device(rhs_leaf, rhs_anc, leaf_inv, leaf_low, couple, tile_cols, anc_inv, anc_low):
    leaf_tiles, tile, _ = leaf_inv.shape
    cols = rhs_leaf.shape[1]
    half = cols // 2
    count = lax.axis_size("row")
    far = count // 2
    decks = lax.axis_size("layer") // 2
    base = leaf_tiles * tile

    msg, anc = call(
        leaf_body, (shape(base, cols), shape(tile, tile)),
        (rhs_leaf, leaf_inv, leaf_low, anc_inv, anc_low), stay=True,
    )
    msgs = gather_row(msg, far)
    ancs = gather_row(anc, far)
    mats = merge(couple, tile_cols, leaf_tiles)
    columns = [pair_swap(mats[i], "row", i) for i in range(1, count)]

    own, other, right = call(
        functools.partial(partial_body, count), [shape(half, tile)] * 3,
        (msg, rhs_anc), (*mats, *msgs[1:]), [pltpu.VMEM((cols, tile), F32)], stay=True,
    )
    part = own + pair_swap(other, "layer", 1)
    total = part
    for k in range(1, decks):
        total = total + pair_swap(part, "layer", 2 * k)
    pieces = gather_row(right - total, far)

    mine, = call(stack_body, [shape(count, tile, tile)], (anc,), ancs[1:], stay=True)
    theirs = pair_swap(mine, "layer", 1)
    z_mine, = call(
        functools.partial(solve_body, count), [shape(count, half, tile)],
        (), (mine, theirs, *pieces),
        [pltpu.VMEM((count, half, tile), F32)] + [pltpu.VMEM((count, tile, tile), F32)] * 2,
        stay=True,
    )
    z_theirs = pair_swap(z_mine, "layer", 1)
    leaf, anc_out = call(
        functools.partial(final_body, count),
        (shape(base, cols), shape(tile, cols)),
        (mats[0], msg, leaf_inv, leaf_low), (z_mine, z_theirs, *columns),
        [pltpu.VMEM((count, cols, tile), F32)],
    )
    return leaf, anc_out


def solution(mesh):
    placed = (
        P(("layer", "row"), None),
        P("row", None),
        P(("layer", "row"), None, None),
        P(("layer", "row"), None, None),
        P(("layer", "row"), None, None),
        P(("layer", "row"), None),
        P("row", None, None),
        P("row", None, None),
    )

    return jax.shard_map(
        per_device,
        mesh=mesh,
        in_specs=placed,
        out_specs=(P(("layer", "row"), None), P("row", None)),
        check_vma=False,
    )
```

profile of v0, /device:TPU:9, one launch (start us, length us, event | category | flops | bytes accessed | tf_op | source)
XLA Modules:
  0.0 89.6 jit_solution(17722727975331668655)
XLA Ops:
  5.0 1.2 %shard_map.95 = (f32[256,128]{1,0:T(8,128)S(1)}, f32[128,128]{1,0:T(8,128)S(1)}) custom-call(f32[256,128]{1,0:T(8,128)S(1)} %copy-done.5, f32[2,128,128]{2,1,0:T(8,128)S(1)} %copy-done.1, f32[1,128,128]{2,1,0:T(8,128)S(1)} %copy-done.3, f32[1,128,128]{2,1,0:T(8,128)S(1)} %copy-done.6, f32[1,128,128]{2,1,0:T(8,128)S(1)} %copy-done.7), custom_call_target="tpu_custom_call" | custom-call | tf_op jit(solution)/shard_map/pallas_call | solution.py:52
  6.3 2.5 %collective-permute-start.3 = (f32[128,128]{1,0:T(8,128)S(1)}, f32[128,128]{1,0:T(8,128)S(1)}, u32[]{:S(2)}, u32[]{:S(2)}) collective-permute-start(f32[128,128]{1,0:T(8,128)S(1)} %get-tuple-element.17.refs_0_), channel_id=1, source_target_pairs={{0,4},{1,5},{2,6},{3,7},{4,0},{5,1},{6,2},{7,3},{8,12},{9,13},{10,... | collective-permute-start | bytes 196616 | tf_op jit(solution)/shard_map/ppermute | solution.py:76
  8.9 1.2 %collective-permute-start = (f32[128,128]{1,0:T(8,128)S(1)}, f32[128,128]{1,0:T(8,128)S(1)}, u32[]{:S(2)}, u32[]{:S(2)}) collective-permute-start(f32[128,128]{1,0:T(8,128)S(1)} %get-tuple-element.17.refs_0_), channel_id=1, source_target_pairs={{0,1},{1,0},{2,3},{3,2},{4,5},{5,4},{6,7},{7,6},{8,9},{9,8},{10,11... | collective-permute-start | bytes 196616 | tf_op jit(solution)/shard_map/ppermute | solution.py:76
  10.6 0.9 %collective-permute-start.9 = (f32[256,128]{1,0:T(8,128)S(1)}, f32[256,128]{1,0:T(8,128)S(1)}, u32[]{:S(2)}, u32[]{:S(2)}) collective-permute-start(f32[256,128]{1,0:T(8,128)S(1)} %get-tuple-element.16.refs_0_.refs_1_), channel_id=1, source_target_pairs={{0,2},{1,3},{2,0},{3,1},{4,6},{5,7},{6,4},{7,5},{8,10},{9,11},{10,... | collective-permute-start | bytes 393224 | tf_op jit(solution)/shard_map/ppermute | solution.py:76
  11.5 2.1 %collective-permute-start.11 = (f32[256,128]{1,0:T(8,128)S(1)}, f32[256,128]{1,0:T(8,128)S(1)}, u32[]{:S(2)}, u32[]{:S(2)}) collective-permute-start(f32[256,128]{1,0:T(8,128)S(1)} %get-tuple-element.16.refs_0_.refs_1_), channel_id=1, source_target_pairs={{0,4},{1,5},{2,6},{3,7},{4,0},{5,1},{6,2},{7,3},{8,12},{9,13},{10,... | collective-permute-start | bytes 393224 | tf_op jit(solution)/shard_map/ppermute | solution.py:76
  14.3 1.3 %collective-permute-start.13 = (f32[256,128]{1,0:T(8,128)S(1)}, f32[256,128]{1,0:T(8,128)S(1)}, u32[]{:S(2)}, u32[]{:S(2)}) collective-permute-start(f32[256,128]{1,0:T(8,128)S(1)} %get-tuple-element.16.refs_0_.refs_1_), channel_id=1, source_target_pairs={{0,6},{1,7},{2,4},{3,5},{4,2},{5,3},{6,0},{7,1},{8,14},{9,15},{10,... | collective-permute-start | bytes 393224 | tf_op jit(solution)/shard_map/ppermute | solution.py:76
  15.6 1.2 %collective-permute-start.4 = (f32[128,128]{1,0:T(8,128)S(1)}, f32[128,128]{1,0:T(8,128)S(1)}, u32[]{:S(2)}, u32[]{:S(2)}) collective-permute-start(f32[128,128]{1,0:T(8,128)S(1)} %collective-permute-done.3.refs_4_), channel_id=1, source_target_pairs={{0,1},{1,0},{2,3},{3,2},{4,5},{5,4},{6,7},{7,6},{8,9},{9,8},{10,11... | collective-permute-start | bytes 196616 | tf_op jit(solution)/shard_map/ppermute | solution.py:76
  17.1 1.6 %collective-permute-done.4.refs_5_ = f32[128,128]{1,0:T(8,128)S(1)} collective-permute-done((f32[128,128]{1,0:T(8,128)S(1)}, f32[128,128]{1,0:T(8,128)S(1)}, u32[]{:S(2)}, u32[]{:S(2)}) %collective-permute-start.4) | collective-permute-done | bytes 65568 | tf_op jit(solution)/shard_map/ppermute | solution.py:76
  18.7 1.5 %collective-permute-done.6.refs_7_ = f32[128,128]{1,0:T(8,128)S(1)} collective-permute-done((f32[128,128]{1,0:T(8,128)S(1)}, f32[128,128]{1,0:T(8,128)S(1)}, u32[]{:S(2)}, u32[]{:S(2)}) %collective-permute-start.6) | collective-permute-done | bytes 65568 | tf_op jit(solution)/shard_map/ppermute | solution.py:76
  20.3 4.4 %collective-permute-start.7 = (f32[8,128,128]{2,1,0:T(8,128)S(1)}, f32[8,128,128]{2,1,0:T(8,128)S(1)}, u32[]{:S(2)}, u32[]{:S(2)}) collective-permute-start(f32[8,128,128]{2,1,0:T(8,128)S(1)} %shard_map.96.refs_0_), channel_id=1, source_target_pairs={{0,8},{8,0},{16,24},{24,16},{1,9},{9,1},{17,25},{25,17},{2,10},{10... | collective-permute-start | bytes 1572872 | tf_op jit(solution)/shard_map/ppermute | solution.py:76
  25.1 1.0 %collective-permute-start.10 = (f32[256,128]{1,0:T(8,128)S(1)}, f32[256,128]{1,0:T(8,128)S(1)}, u32[]{:S(2)}, u32[]{:S(2)}) collective-permute-start(f32[256,128]{1,0:T(8,128)S(1)} %collective-permute-done.9.refs_11_), channel_id=1, source_target_pairs={{0,1},{1,0},{2,3},{3,2},{4,5},{5,4},{6,7},{7,6},{8,9},{9,8},{10,11... | collective-permute-start | bytes 393224 | tf_op jit(solution)/shard_map/ppermute | solution.py:76
  26.6 1.0 %collective-permute-start.14 = (f32[256,128]{1,0:T(8,128)S(1)}, f32[256,128]{1,0:T(8,128)S(1)}, u32[]{:S(2)}, u32[]{:S(2)}) collective-permute-start(f32[256,128]{1,0:T(8,128)S(1)} %collective-permute-done.13.refs_15_), channel_id=1, source_target_pairs={{0,1},{1,0},{2,3},{3,2},{4,5},{5,4},{6,7},{7,6},{8,9},{9,8},{10,11... | collective-permute-start | bytes 393224 | tf_op jit(solution)/shard_map/ppermute | solution.py:76
  27.7 3.4 %copy-done = f32[128,128,128]{2,1,0:T(8,128)S(1)} copy-done((f32[128,128,128]{2,1,0:T(8,128)S(1)}, f32[128,128,128]{2,1,0:T(8,128)}, u32[]{:S(2)}) %copy-start) | copy-done | bytes 8388632
  31.7 2.4 %merge.1 = (f32[2,128,128]{2,1,0:T(8,128)S(1)}, f32[2,128,128]{2,1,0:T(8,128)S(1)}, f32[2,128,128]{2,1,0:T(8,128)S(1)}, f32[2,128,128]{2,1,0:T(8,128)S(1)}, f32[...) custom-call(s32[1,128]{1,0:T(1,128)S(1)} %copy-done.9, ...), custom_call_target="tpu_custom_call" | custom-call | tf_op jit(solution)/shard_map/merge/pallas_call | solution.py:138
  34.2 1.1 %collective-permute-done.12.refs_14_ = f32[256,128]{1,0:T(8,128)S(1)} collective-permute-done((f32[256,128]{1,0:T(8,128)S(1)}, f32[256,128]{1,0:T(8,128)S(1)}, u32[]{:S(2)}, u32[]{:S(2)}) %collective-permute-start.12) | collective-permute-done | bytes 131104 | tf_op jit(solution)/shard_map/ppermute | solution.py:76
  35.3 2.8 %collective-permute-done.14.refs_16_ = f32[256,128]{1,0:T(8,128)S(1)} collective-permute-done((f32[256,128]{1,0:T(8,128)S(1)}, f32[256,128]{1,0:T(8,128)S(1)}, u32[]{:S(2)}, u32[]{:S(2)}) %collective-permute-start.14) | collective-permute-done | bytes 131104 | tf_op jit(solution)/shard_map/ppermute | solution.py:76
  38.1 1.1 %shard_map.97 = (f32[64,128]{1,0:T(8,128)S(1)}, f32[64,128]{1,0:T(8,128)S(1)}, f32[64,128]{1,0:T(8,128)S(1)}) custom-call(f32[256,128]{1,0:T(8,128)S(1)} %get-tuple-element.16.refs_0_.refs_1_, f32[128,128]{1,0:T(8,128)S(1)} %copy-done.8, f32[2,128,128]{2,1,0:T(8,128)S(1)} %get-tuple-element.15.refs_2_.refs_0_, f32[2,128,128]{2,1,0:T(8,128)S(1)} %get-tuple-element.18.refs_3_, ...), custom_call_target="tpu_custom_call" | custom-call | tf_op jit(solution)/shard_map/pallas_call | solution.py:52
  39.2 1.0 %collective-permute-start.15 = (f32[64,128]{1,0:T(8,128)S(1)}, f32[64,128]{1,0:T(8,128)S(1)}, u32[]{:S(2)}, u32[]{:S(2)}) collective-permute-start(f32[64,128]{1,0:T(8,128)S(1)} %get-tuple-element.27), channel_id=1, source_target_pairs={{0,8},{8,0},{16,24},{24,16},{1,9},{9,1},{17,25},{25,17},{2,10},{10... | collective-permute-start | bytes 98312 | tf_op jit(solution)/shard_map/ppermute | solution.py:76
  41.1 1.2 %collective-permute-start.16 = (f32[64,128]{1,0:T(8,128)S(1)}, f32[64,128]{1,0:T(8,128)S(1)}, u32[]{:S(2)}, u32[]{:S(2)}) collective-permute-start(f32[64,128]{1,0:T(8,128)S(1)} %add.6), channel_id=1, source_target_pairs={{0,16},{8,24},{16,0},{24,8},{1,17},{9,25},{17,1},{25,9},{2,18},{10... | collective-permute-start | bytes 98312 | tf_op jit(solution)/shard_map/ppermute | solution.py:76
  42.3 1.5 %collective-permute-done.16 = f32[64,128]{1,0:T(8,128)S(1)} collective-permute-done((f32[64,128]{1,0:T(8,128)S(1)}, f32[64,128]{1,0:T(8,128)S(1)}, u32[]{:S(2)}, u32[]{:S(2)}) %collective-permute-start.16) | collective-permute-done | bytes 32800 | tf_op jit(solution)/shard_map/ppermute | solution.py:76
  44.3 1.7 %collective-permute-start.20 = (f32[64,128]{1,0:T(8,128)S(1)}, f32[64,128]{1,0:T(8,128)S(1)}, u32[]{:S(2)}, u32[]{:S(2)}) collective-permute-start(f32[64,128]{1,0:T(8,128)S(1)} %add_subtract_fusion.refs_2_), channel_id=1, source_target_pairs={{0,4},{1,5},{2,6},{3,7},{4,0},{5,1},{6,2},{7,3},{8,12},{9,13},{10,... | collective-permute-start | bytes 98312 | tf_op jit(solution)/shard_map/ppermute | solution.py:76
  47.0 1.0 %collective-permute-start.19 = (f32[64,128]{1,0:T(8,128)S(1)}, f32[64,128]{1,0:T(8,128)S(1)}, u32[]{:S(2)}, u32[]{:S(2)}) collective-permute-start(f32[64,128]{1,0:T(8,128)S(1)} %collective-permute-done.18.refs_4_), channel_id=1, source_target_pairs={{0,1},{1,0},{2,3},{3,2},{4,5},{5,4},{6,7},{7,6},{8,9},{9,8},{10,11... | collective-permute-start | bytes 98312 | tf_op jit(solution)/shard_map/ppermute | solution.py:76
  50.5 2.9 %collective-permute-start.26 = (f32[2,128,128]{2,1,0:T(8,128)S(1)}, f32[2,128,128]{2,1,0:T(8,128)S(1)}, u32[]{:S(2)}, u32[]{:S(2)}) collective-permute-start(f32[2,128,128]{2,1,0:T(8,128)S(1)} %get-tuple-element.19.refs_4_), channel_id=1, source_target_pairs={{0,2},{1,3},{2,0},{3,1},{4,6},{5,7},{6,4},{7,5},{8,10},{9,11},{10,... | collective-permute-start | bytes 393224 | tf_op jit(solution)/shard_map/ppermute | solution.py:76
  53.6 2.7 %shard_map.98.refs_4_ = f32[8,64,128]{2,1,0:T(8,128)S(1)} custom-call(f32[8,128,128]{2,1,0:T(8,128)S(1)} %shard_map.96.refs_0_, f32[8,128,128]{2,1,0:T(8,128)S(1)} %collective-permute-done.7.refs_1_, f32[64,128]{1,0:T(8,128)S(1)} %add_subtract_fusion.refs_2_, f32[64,128]{1,0:T(8,128)S(1)} %collective-permute-done.17.refs_3_, ...), custom_call_target="tpu_custom_call" | custom-call | tf_op jit(solution)/shard_map/pallas_call | solution.py:52
  56.3 3.8 %collective-permute-start.24 = (f32[8,64,128]{2,1,0:T(8,128)S(1)}, f32[8,64,128]{2,1,0:T(8,128)S(1)}, u32[]{:S(2)}, u32[]{:S(2)}) collective-permute-start(f32[8,64,128]{2,1,0:T(8,128)S(1)} %shard_map.98.refs_4_), channel_id=1, source_target_pairs={{0,8},{8,0},{16,24},{24,16},{1,9},{9,1},{17,25},{25,17},{2,10},{10... | collective-permute-start | bytes 786440 | tf_op jit(solution)/shard_map/ppermute | solution.py:76
  60.1 2.3 %collective-permute-start.28 = (f32[2,128,128]{2,1,0:T(8,128)S(1)}, f32[2,128,128]{2,1,0:T(8,128)S(1)}, u32[]{:S(2)}, u32[]{:S(2)}) collective-permute-start(f32[2,128,128]{2,1,0:T(8,128)S(1)} %get-tuple-element.21.refs_6_), channel_id=1, source_target_pairs={{0,4},{1,5},{2,6},{3,7},{4,0},{5,1},{6,2},{7,3},{8,12},{9,13},{10,... | collective-permute-start | bytes 393224 | tf_op jit(solution)/shard_map/ppermute | solution.py:76
  63.2 1.1 %collective-permute-start.30 = (f32[2,128,128]{2,1,0:T(8,128)S(1)}, f32[2,128,128]{2,1,0:T(8,128)S(1)}, u32[]{:S(2)}, u32[]{:S(2)}) collective-permute-start(f32[2,128,128]{2,1,0:T(8,128)S(1)} %get-tuple-element.23.refs_8_), channel_id=1, source_target_pairs={{0,6},{1,7},{2,4},{3,5},{4,2},{5,3},{6,0},{7,1},{8,14},{9,15},{10,... | collective-permute-start | bytes 393224 | tf_op jit(solution)/shard_map/ppermute | solution.py:76
  64.9 11.9 %collective-permute-done.28.refs_9_ = f32[2,128,128]{2,1,0:T(8,128)S(1)} collective-permute-done((f32[2,128,128]{2,1,0:T(8,128)S(1)}, f32[2,128,128]{2,1,0:T(8,128)S(1)}, u32[]{:S(2)}, u32[]{:S(2)}) %collective-permute-start.28) | collective-permute-done | bytes 131104 | tf_op jit(solution)/shard_map/ppermute | solution.py:76
  76.7 2.8 %collective-permute-done.29.refs_10_ = f32[2,128,128]{2,1,0:T(8,128)S(1)} collective-permute-done((f32[2,128,128]{2,1,0:T(8,128)S(1)}, f32[2,128,128]{2,1,0:T(8,128)S(1)}, u32[]{:S(2)}, u32[]{:S(2)}) %collective-permute-start.29) | collective-permute-done | bytes 131104 | tf_op jit(solution)/shard_map/ppermute | solution.py:76
  79.6 3.8 %collective-permute-done.30.refs_11_ = f32[2,128,128]{2,1,0:T(8,128)S(1)} collective-permute-done((f32[2,128,128]{2,1,0:T(8,128)S(1)}, f32[2,128,128]{2,1,0:T(8,128)S(1)}, u32[]{:S(2)}, u32[]{:S(2)}) %collective-permute-start.30) | collective-permute-done | bytes 131104 | tf_op jit(solution)/shard_map/ppermute | solution.py:76
  83.3 3.6 %collective-permute-done.31.refs_12_ = f32[2,128,128]{2,1,0:T(8,128)S(1)} collective-permute-done((f32[2,128,128]{2,1,0:T(8,128)S(1)}, f32[2,128,128]{2,1,0:T(8,128)S(1)}, u32[]{:S(2)}, u32[]{:S(2)}) %collective-permute-start.31) | collective-permute-done | bytes 131104 | tf_op jit(solution)/shard_map/ppermute | solution.py:76
  86.9 2.7 %shard_map.99 = (f32[256,128]{1,0:T(8,128)}, f32[128,128]{1,0:T(8,128)}) custom-call(f32[2,128,128]{2,1,0:T(8,128)S(1)} %get-tuple-element.15.refs_2_.refs_0_, f32[256,128]{1,0:T(8,128)S(1)} %get-tuple-element.16.refs_0_.refs_1_, f32[2,128,128]{2,1,0:T(8,128)S(1)} %copy-done.2, f32[1,128,128]{2,1,0:T(8,128)S(1)} %copy-done.4, ...), custom_call_target="tpu_custom_call" | custom-call | tf_op jit(solution)/shard_map/pallas_call | solution.py:52
  (60 shorter events, 13.9 us)
Async XLA Ops:
  6.2 3.9 %collective-permute-start.1 = (f32[128,128]{1,0:T(8,128)S(1)}, f32[128,128]{1,0:T(8,128)S(1)}, u32[]{:S(2)}, u32[]{:S(2)}) collective-permute-start(f32[128,128]{1,0:T(8,128)S(1)} %get-tuple-element.17.refs_0_), channel_id=1, source_target_pairs={{0,2},{1,3},{2,0},{3,1},{4,6},{5,7},{6,4},{7,5},{8,10},{9,11},{10,... | collective-permute-start | bytes 196616 | tf_op jit(solution)/shard_map/ppermute | solution.py:76
  6.3 5.2 %collective-permute-start.3 = (f32[128,128]{1,0:T(8,128)S(1)}, f32[128,128]{1,0:T(8,128)S(1)}, u32[]{:S(2)}, u32[]{:S(2)}) collective-permute-start(f32[128,128]{1,0:T(8,128)S(1)} %get-tuple-element.17.refs_0_), channel_id=1, source_target_pairs={{0,4},{1,5},{2,6},{3,7},{4,0},{5,1},{6,2},{7,3},{8,12},{9,13},{10,... | collective-permute-start | bytes 196616 | tf_op jit(solution)/shard_map/ppermute | solution.py:76
  8.7 5.6 %collective-permute-start.5 = (f32[128,128]{1,0:T(8,128)S(1)}, f32[128,128]{1,0:T(8,128)S(1)}, u32[]{:S(2)}, u32[]{:S(2)}) collective-permute-start(f32[128,128]{1,0:T(8,128)S(1)} %get-tuple-element.17.refs_0_), channel_id=1, source_target_pairs={{0,6},{1,7},{2,4},{3,5},{4,2},{5,3},{6,0},{7,1},{8,14},{9,15},{10,... | collective-permute-start | bytes 196616 | tf_op jit(solution)/shard_map/ppermute | solution.py:76
  8.9 6.7 %collective-permute-start = (f32[128,128]{1,0:T(8,128)S(1)}, f32[128,128]{1,0:T(8,128)S(1)}, u32[]{:S(2)}, u32[]{:S(2)}) collective-permute-start(f32[128,128]{1,0:T(8,128)S(1)} %get-tuple-element.17.refs_0_), channel_id=1, source_target_pairs={{0,1},{1,0},{2,3},{3,2},{4,5},{5,4},{6,7},{7,6},{8,9},{9,8},{10,11... | collective-permute-start | bytes 196616 | tf_op jit(solution)/shard_map/ppermute | solution.py:76
  10.1 6.6 %collective-permute-start.2 = (f32[128,128]{1,0:T(8,128)S(1)}, f32[128,128]{1,0:T(8,128)S(1)}, u32[]{:S(2)}, u32[]{:S(2)}) collective-permute-start(f32[128,128]{1,0:T(8,128)S(1)} %collective-permute-done.1.refs_2_), channel_id=1, source_target_pairs={{0,1},{1,0},{2,3},{3,2},{4,5},{5,4},{6,7},{7,6},{8,9},{9,8},{10,11... | collective-permute-start | bytes 196616 | tf_op jit(solution)/shard_map/ppermute | solution.py:76
  10.6 14.6 %collective-permute-start.9 = (f32[256,128]{1,0:T(8,128)S(1)}, f32[256,128]{1,0:T(8,128)S(1)}, u32[]{:S(2)}, u32[]{:S(2)}) collective-permute-start(f32[256,128]{1,0:T(8,128)S(1)} %get-tuple-element.16.refs_0_.refs_1_), channel_id=1, source_target_pairs={{0,2},{1,3},{2,0},{3,1},{4,6},{5,7},{6,4},{7,5},{8,10},{9,11},{10,... | collective-permute-start | bytes 393224 | tf_op jit(solution)/shard_map/ppermute | solution.py:76
  11.5 14.7 %collective-permute-start.11 = (f32[256,128]{1,0:T(8,128)S(1)}, f32[256,128]{1,0:T(8,128)S(1)}, u32[]{:S(2)}, u32[]{:S(2)}) collective-permute-start(f32[256,128]{1,0:T(8,128)S(1)} %get-tuple-element.16.refs_0_.refs_1_), channel_id=1, source_target_pairs={{0,4},{1,5},{2,6},{3,7},{4,0},{5,1},{6,2},{7,3},{8,12},{9,13},{10,... | collective-permute-start | bytes 393224 | tf_op jit(solution)/shard_map/ppermute | solution.py:76
  14.3 12.3 %collective-permute-start.13 = (f32[256,128]{1,0:T(8,128)S(1)}, f32[256,128]{1,0:T(8,128)S(1)}, u32[]{:S(2)}, u32[]{:S(2)}) collective-permute-start(f32[256,128]{1,0:T(8,128)S(1)} %get-tuple-element.16.refs_0_.refs_1_), channel_id=1, source_target_pairs={{0,6},{1,7},{2,4},{3,5},{4,2},{5,3},{6,0},{7,1},{8,14},{9,15},{10,... | collective-permute-start | bytes 393224 | tf_op jit(solution)/shard_map/ppermute | solution.py:76
  15.6 3.1 %collective-permute-start.4 = (f32[128,128]{1,0:T(8,128)S(1)}, f32[128,128]{1,0:T(8,128)S(1)}, u32[]{:S(2)}, u32[]{:S(2)}) collective-permute-start(f32[128,128]{1,0:T(8,128)S(1)} %collective-permute-done.3.refs_4_), channel_id=1, source_target_pairs={{0,1},{1,0},{2,3},{3,2},{4,5},{5,4},{6,7},{7,6},{8,9},{9,8},{10,11... | collective-permute-start | bytes 196616 | tf_op jit(solution)/shard_map/ppermute | solution.py:76
  16.7 3.4 %collective-permute-start.6 = (f32[128,128]{1,0:T(8,128)S(1)}, f32[128,128]{1,0:T(8,128)S(1)}, u32[]{:S(2)}, u32[]{:S(2)}) collective-permute-start(f32[128,128]{1,0:T(8,128)S(1)} %collective-permute-done.5.refs_6_), channel_id=1, source_target_pairs={{0,1},{1,0},{2,3},{3,2},{4,5},{5,4},{6,7},{7,6},{8,9},{9,8},{10,11... | collective-permute-start | bytes 196616 | tf_op jit(solution)/shard_map/ppermute | solution.py:76
  20.3 33.3 %collective-permute-start.7 = (f32[8,128,128]{2,1,0:T(8,128)S(1)}, f32[8,128,128]{2,1,0:T(8,128)S(1)}, u32[]{:S(2)}, u32[]{:S(2)}) collective-permute-start(f32[8,128,128]{2,1,0:T(8,128)S(1)} %shard_map.96.refs_0_), channel_id=1, source_target_pairs={{0,8},{8,0},{16,24},{24,16},{1,9},{9,1},{17,25},{25,17},{2,10},{10... | collective-permute-start | bytes 1572872 | tf_op jit(solution)/shard_map/ppermute | solution.py:76
  24.7 9.4 %collective-permute-start.8 = (f32[256,128]{1,0:T(8,128)S(1)}, f32[256,128]{1,0:T(8,128)S(1)}, u32[]{:S(2)}, u32[]{:S(2)}) collective-permute-start(f32[256,128]{1,0:T(8,128)S(1)} %get-tuple-element.16.refs_0_.refs_1_), channel_id=1, source_target_pairs={{0,1},{1,0},{2,3},{3,2},{4,5},{5,4},{6,7},{7,6},{8,9},{9,8},{10,11... | collective-permute-start | bytes 393224 | tf_op jit(solution)/shard_map/ppermute | solution.py:76
  25.1 9.0 %collective-permute-start.10 = (f32[256,128]{1,0:T(8,128)S(1)}, f32[256,128]{1,0:T(8,128)S(1)}, u32[]{:S(2)}, u32[]{:S(2)}) collective-permute-start(f32[256,128]{1,0:T(8,128)S(1)} %collective-permute-done.9.refs_11_), channel_id=1, source_target_pairs={{0,1},{1,0},{2,3},{3,2},{4,5},{5,4},{6,7},{7,6},{8,9},{9,8},{10,11... | collective-permute-start | bytes 393224 | tf_op jit(solution)/shard_map/ppermute | solution.py:76
  26.2 9.1 %collective-permute-start.12 = (f32[256,128]{1,0:T(8,128)S(1)}, f32[256,128]{1,0:T(8,128)S(1)}, u32[]{:S(2)}, u32[]{:S(2)}) collective-permute-start(f32[256,128]{1,0:T(8,128)S(1)} %collective-permute-done.11.refs_13_), channel_id=1, source_target_pairs={{0,1},{1,0},{2,3},{3,2},{4,5},{5,4},{6,7},{7,6},{8,9},{9,8},{10,11... | collective-permute-start | bytes 393224 | tf_op jit(solution)/shard_map/ppermute | solution.py:76
  26.6 11.5 %collective-permute-start.14 = (f32[256,128]{1,0:T(8,128)S(1)}, f32[256,128]{1,0:T(8,128)S(1)}, u32[]{:S(2)}, u32[]{:S(2)}) collective-permute-start(f32[256,128]{1,0:T(8,128)S(1)} %collective-permute-done.13.refs_15_), channel_id=1, source_target_pairs={{0,1},{1,0},{2,3},{3,2},{4,5},{5,4},{6,7},{7,6},{8,9},{9,8},{10,11... | collective-permute-start | bytes 393224 | tf_op jit(solution)/shard_map/ppermute | solution.py:76
  39.2 1.9 %collective-permute-start.15 = (f32[64,128]{1,0:T(8,128)S(1)}, f32[64,128]{1,0:T(8,128)S(1)}, u32[]{:S(2)}, u32[]{:S(2)}) collective-permute-start(f32[64,128]{1,0:T(8,128)S(1)} %get-tuple-element.27), channel_id=1, source_target_pairs={{0,8},{8,0},{16,24},{24,16},{1,9},{9,1},{17,25},{25,17},{2,10},{10... | collective-permute-start | bytes 98312 | tf_op jit(solution)/shard_map/ppermute | solution.py:76
  41.1 2.8 %collective-permute-start.16 = (f32[64,128]{1,0:T(8,128)S(1)}, f32[64,128]{1,0:T(8,128)S(1)}, u32[]{:S(2)}, u32[]{:S(2)}) collective-permute-start(f32[64,128]{1,0:T(8,128)S(1)} %add.6), channel_id=1, source_target_pairs={{0,16},{8,24},{16,0},{24,8},{1,17},{9,25},{17,1},{25,9},{2,18},{10... | collective-permute-start | bytes 98312 | tf_op jit(solution)/shard_map/ppermute | solution.py:76
  43.8 3.1 %collective-permute-start.18 = (f32[64,128]{1,0:T(8,128)S(1)}, f32[64,128]{1,0:T(8,128)S(1)}, u32[]{:S(2)}, u32[]{:S(2)}) collective-permute-start(f32[64,128]{1,0:T(8,128)S(1)} %add_subtract_fusion.refs_2_), channel_id=1, source_target_pairs={{0,2},{1,3},{2,0},{3,1},{4,6},{5,7},{6,4},{7,5},{8,10},{9,11},{10,... | collective-permute-start | bytes 98312 | tf_op jit(solution)/shard_map/ppermute | solution.py:76
  44.3 3.8 %collective-permute-start.20 = (f32[64,128]{1,0:T(8,128)S(1)}, f32[64,128]{1,0:T(8,128)S(1)}, u32[]{:S(2)}, u32[]{:S(2)}) collective-permute-start(f32[64,128]{1,0:T(8,128)S(1)} %add_subtract_fusion.refs_2_), channel_id=1, source_target_pairs={{0,4},{1,5},{2,6},{3,7},{4,0},{5,1},{6,2},{7,3},{8,12},{9,13},{10,... | collective-permute-start | bytes 98312 | tf_op jit(solution)/shard_map/ppermute | solution.py:76
  46.1 2.9 %collective-permute-start.22 = (f32[64,128]{1,0:T(8,128)S(1)}, f32[64,128]{1,0:T(8,128)S(1)}, u32[]{:S(2)}, u32[]{:S(2)}) collective-permute-start(f32[64,128]{1,0:T(8,128)S(1)} %add_subtract_fusion.refs_2_), channel_id=1, source_target_pairs={{0,6},{1,7},{2,4},{3,5},{4,2},{5,3},{6,0},{7,1},{8,14},{9,15},{10,... | collective-permute-start | bytes 98312 | tf_op jit(solution)/shard_map/ppermute | solution.py:76
  46.6 3.0 %collective-permute-start.17 = (f32[64,128]{1,0:T(8,128)S(1)}, f32[64,128]{1,0:T(8,128)S(1)}, u32[]{:S(2)}, u32[]{:S(2)}) collective-permute-start(f32[64,128]{1,0:T(8,128)S(1)} %add_subtract_fusion.refs_2_), channel_id=1, source_target_pairs={{0,1},{1,0},{2,3},{3,2},{4,5},{5,4},{6,7},{7,6},{8,9},{9,8},{10,11... | collective-permute-start | bytes 98312 | tf_op jit(solution)/shard_map/ppermute | solution.py:76
  47.0 3.5 %collective-permute-start.19 = (f32[64,128]{1,0:T(8,128)S(1)}, f32[64,128]{1,0:T(8,128)S(1)}, u32[]{:S(2)}, u32[]{:S(2)}) collective-permute-start(f32[64,128]{1,0:T(8,128)S(1)} %collective-permute-done.18.refs_4_), channel_id=1, source_target_pairs={{0,1},{1,0},{2,3},{3,2},{4,5},{5,4},{6,7},{7,6},{8,9},{9,8},{10,11... | collective-permute-start | bytes 98312 | tf_op jit(solution)/shard_map/ppermute | solution.py:76
  48.1 5.2 %collective-permute-start.21 = (f32[64,128]{1,0:T(8,128)S(1)}, f32[64,128]{1,0:T(8,128)S(1)}, u32[]{:S(2)}, u32[]{:S(2)}) collective-permute-start(f32[64,128]{1,0:T(8,128)S(1)} %collective-permute-done.20.refs_6_), channel_id=1, source_target_pairs={{0,1},{1,0},{2,3},{3,2},{4,5},{5,4},{6,7},{7,6},{8,9},{9,8},{10,11... | collective-permute-start | bytes 98312 | tf_op jit(solution)/shard_map/ppermute | solution.py:76
  49.0 4.6 %collective-permute-start.23 = (f32[64,128]{1,0:T(8,128)S(1)}, f32[64,128]{1,0:T(8,128)S(1)}, u32[]{:S(2)}, u32[]{:S(2)}) collective-permute-start(f32[64,128]{1,0:T(8,128)S(1)} %collective-permute-done.22.refs_8_), channel_id=1, source_target_pairs={{0,1},{1,0},{2,3},{3,2},{4,5},{5,4},{6,7},{7,6},{8,9},{9,8},{10,11... | collective-permute-start | bytes 98312 | tf_op jit(solution)/shard_map/ppermute | solution.py:76
  49.6 12.8 %collective-permute-start.25 = (f32[2,128,128]{2,1,0:T(8,128)S(1)}, f32[2,128,128]{2,1,0:T(8,128)S(1)}, u32[]{:S(2)}, u32[]{:S(2)}) collective-permute-start(f32[2,128,128]{2,1,0:T(8,128)S(1)} %get-tuple-element.18.refs_3_), channel_id=1, source_target_pairs={{0,1},{1,0},{2,3},{3,2},{4,5},{5,4},{6,7},{7,6},{8,9},{9,8},{10,11... | collective-permute-start | bytes 393224 | tf_op jit(solution)/shard_map/ppermute | solution.py:76
  50.5 12.8 %collective-permute-start.26 = (f32[2,128,128]{2,1,0:T(8,128)S(1)}, f32[2,128,128]{2,1,0:T(8,128)S(1)}, u32[]{:S(2)}, u32[]{:S(2)}) collective-permute-start(f32[2,128,128]{2,1,0:T(8,128)S(1)} %get-tuple-element.19.refs_4_), channel_id=1, source_target_pairs={{0,2},{1,3},{2,0},{3,1},{4,6},{5,7},{6,4},{7,5},{8,10},{9,11},{10,... | collective-permute-start | bytes 393224 | tf_op jit(solution)/shard_map/ppermute | solution.py:76
  53.4 11.0 %collective-permute-start.27 = (f32[2,128,128]{2,1,0:T(8,128)S(1)}, f32[2,128,128]{2,1,0:T(8,128)S(1)}, u32[]{:S(2)}, u32[]{:S(2)}) collective-permute-start(f32[2,128,128]{2,1,0:T(8,128)S(1)} %get-tuple-element.20.refs_5_), channel_id=1, source_target_pairs={{0,3},{1,2},{2,1},{3,0},{4,7},{5,6},{6,5},{7,4},{8,11},{9,10},{10,... | collective-permute-start | bytes 393224 | tf_op jit(solution)/shard_map/ppermute | solution.py:76
  56.3 30.6 %collective-permute-start.24 = (f32[8,64,128]{2,1,0:T(8,128)S(1)}, f32[8,64,128]{2,1,0:T(8,128)S(1)}, u32[]{:S(2)}, u32[]{:S(2)}) collective-permute-start(f32[8,64,128]{2,1,0:T(8,128)S(1)} %shard_map.98.refs_4_), channel_id=1, source_target_pairs={{0,8},{8,0},{16,24},{24,16},{1,9},{9,1},{17,25},{25,17},{2,10},{10... | collective-permute-start | bytes 786440 | tf_op jit(solution)/shard_map/ppermute | solution.py:76
  60.1 16.6 %collective-permute-start.28 = (f32[2,128,128]{2,1,0:T(8,128)S(1)}, f32[2,128,128]{2,1,0:T(8,128)S(1)}, u32[]{:S(2)}, u32[]{:S(2)}) collective-permute-start(f32[2,128,128]{2,1,0:T(8,128)S(1)} %get-tuple-element.21.refs_6_), channel_id=1, source_target_pairs={{0,4},{1,5},{2,6},{3,7},{4,0},{5,1},{6,2},{7,3},{8,12},{9,13},{10,... | collective-permute-start | bytes 393224 | tf_op jit(solution)/shard_map/ppermute | solution.py:76
  62.4 17.2 %collective-permute-start.29 = (f32[2,128,128]{2,1,0:T(8,128)S(1)}, f32[2,128,128]{2,1,0:T(8,128)S(1)}, u32[]{:S(2)}, u32[]{:S(2)}) collective-permute-start(f32[2,128,128]{2,1,0:T(8,128)S(1)} %get-tuple-element.22.refs_7_), channel_id=1, source_target_pairs={{0,5},{1,4},{2,7},{3,6},{4,1},{5,0},{6,3},{7,2},{8,13},{9,12},{10,... | collective-permute-start | bytes 393224 | tf_op jit(solution)/shard_map/ppermute | solution.py:76
  63.2 20.1 %collective-permute-start.30 = (f32[2,128,128]{2,1,0:T(8,128)S(1)}, f32[2,128,128]{2,1,0:T(8,128)S(1)}, u32[]{:S(2)}, u32[]{:S(2)}) collective-permute-start(f32[2,128,128]{2,1,0:T(8,128)S(1)} %get-tuple-element.23.refs_8_), channel_id=1, source_target_pairs={{0,6},{1,7},{2,4},{3,5},{4,2},{5,3},{6,0},{7,1},{8,14},{9,15},{10,... | collective-permute-start | bytes 393224 | tf_op jit(solution)/shard_map/ppermute | solution.py:76
  64.4 22.5 %collective-permute-start.31 = (f32[2,128,128]{2,1,0:T(8,128)S(1)}, f32[2,128,128]{2,1,0:T(8,128)S(1)}, u32[]{:S(2)}, u32[]{:S(2)}) collective-permute-start(f32[2,128,128]{2,1,0:T(8,128)S(1)} %get-tuple-element.24.refs_9_), channel_id=1, source_target_pairs={{0,7},{1,6},{2,5},{3,4},{4,3},{5,2},{6,1},{7,0},{8,15},{9,14},{10,... | collective-permute-start | bytes 393224 | tf_op jit(solution)/shard_map/ppermute | solution.py:76
  (10 other events, 205.4 us)
where the time goes:
time: 89.9 us; the launch traced here: 89.6 us
  starting transfers between devices  37.5 us (42%)
  waiting for transfers between devices  32.8 us (36%)
  Pallas kernels  10.2 us (11%)
  local copies, waits for them, and re-layouts  8.36 us (9%)
    ppermute x32, starting transfers between devices, pair_swap(): return lax.ppermute(value, axis, [(i, i ^ distance) for i in range(count)])  37.5 us
    ppermute x32, waiting for transfers between devices, pair_swap(): return lax.ppermute(value, axis, [(i, i ^ distance) for i in range(count)])  32.8 us
    unnamed x20, local copies, waits for them, and re-layouts  8.36 us
    pallas_call x5, Pallas kernels, call(): pl.pallas_call(body, out_shape=list(outs), compiler_params=room(scratch,...  7.74 us
    pallas_call x1, Pallas kernels, merge(): pl.pallas_call(functools.partial(merge_body, leaf_tiles, chunk), name='me...  2.45 us
  transfers between devices with their start and end apart: 32, of which 13 were waited for; matrix products, arithmetic and copies ran while one was open for 0% of the time, Pallas kernels for 7%

commit v1 on v0

v1 whole, which is shorter than its diff:
```python
import functools
import math

import jax
import jax.numpy as jnp
from jax import lax
from jax.experimental import pallas as pl
from jax.experimental.pallas import tpu as pltpu
from jax.sharding import PartitionSpec as P


F32 = jnp.float32
VM = pl.BlockSpec(memory_space=pltpu.VMEM)
HB = pl.BlockSpec(memory_space=pltpu.HBM)
SM = pl.BlockSpec(memory_space=pltpu.SMEM)


def split(value, axis):
    high = value.astype(jnp.bfloat16)
    low = (value - high.astype(F32)).astype(jnp.bfloat16)
    return jnp.concatenate([high, low], axis=axis)


def spread(left, wide):
    rows, width = left.shape[0], wide.shape[1] // 2
    out = jnp.dot(split(left, 0), wide, preferred_element_type=F32)
    cross = out[:rows, width:] + out[rows:, :width]
    return out[:rows, :width] + (cross + out[rows:, width:])


def dot(left, right):
    return spread(left, split(right, 1))


def shape(*dims, dtype=F32):
    return jax.ShapeDtypeStruct(dims, dtype)


def room(scratch, outs=()):
    arrays = [v for v in [*scratch, *outs] if v.dtype in (F32, jnp.bfloat16)]
    size = sum(math.prod(v.shape) * jnp.dtype(v.dtype).itemsize for v in arrays)
    return pltpu.CompilerParams(vmem_limit_bytes=2 * size + (6 << 20))


def call(body, outs, far=(), arrived=(), scratch=(), stay=False):
    far = [pltpu.with_memory_space_constraint(v, pltpu.HBM) for v in far]
    arrived = [pltpu.with_memory_space_constraint(v, pltpu.VMEM) for v in arrived]
    if stay:
        outs = [pltpu.VMEM(o.shape, o.dtype) for o in outs]
    copies = [pltpu.VMEM(v.shape, v.dtype) for v in far]
    if far:
        copies.append(pltpu.SemaphoreType.DMA((len(far),)))
    scratch = copies + list(scratch)
    return pl.pallas_call(
        body, out_shape=list(outs), compiler_params=room(scratch, outs),
        in_specs=[HB] * len(far) + [VM] * len(arrived),
        out_specs=[VM] * len(outs), scratch_shapes=scratch,
    )(*far, *arrived)


def fetch(sources, copies):
    started = [
        pltpu.make_async_copy(source, target, copies[len(sources)].at[i])
        for i, (source, target) in enumerate(zip(sources, copies))
    ]
    for copy in started:
        copy.start()

    def ready(i):
        started[i].wait()
        return copies[i]

    return ready


def pair_swap(value, axis, distance):
    count = lax.axis_size(axis)
    return lax.ppermute(value, axis, [(i, i ^ distance) for i in range(count)])


def leaf_body(*refs):
    ready = fetch(refs[:6], refs[8:])
    inv_far, (msg, right) = refs[1], refs[6:8]
    buf = refs[-1]
    tile = msg.shape[1]
    tiles = inv_far.shape[0]
    half = tile // 2
    share = tile // lax.axis_size("layer")
    base = tiles * tile
    own = pl.multiple_of(lax.axis_index("layer") * share, share)
    start = pl.multiple_of(lax.axis_index("layer") % 2 * half, half)
    rhs, inv, low = ready(0), ready(1), ready(2)
    above = None
    for t in range(tiles):
        source = rhs[t * tile:(t + 1) * tile, :]
        if t > 0:
            source = source - dot(low[t - 1], above)
        above = dot(inv[t], source)
        msg[t * tile:(t + 1) * tile, :] = above
    msg[base:base + share, :] = ready(3)[0, pl.ds(own, share), :]
    msg[base + share:, :] = ready(4)[0, pl.ds(own, share), :]
    buf[...] = ready(5)[...].T
    right[...] = buf[pl.ds(start, half), :]


def merge_body(leaf_tiles, chunk, cols_far, couple, *rest):
    place = lax.axis_index("row")
    outs, (buf, acc_a, acc_b, cols, sems) = rest[:-5], rest[-5:]
    parts = couple.shape[0] // chunk
    table = pltpu.make_async_copy(cols_far, cols, sems.at[parts])
    table.start()
    started = [
        pltpu.make_async_copy(
            couple.at[pl.ds(i * chunk, chunk)], buf.at[pl.ds(i * chunk, chunk)], sems.at[i])
        for i in range(parts)
    ]
    for copy in started:
        copy.start()
    acc_a[...] = jnp.zeros_like(acc_a)
    acc_b[...] = jnp.zeros_like(acc_b)
    table.wait()

    def add(acc, k):
        col = cols[0, k]
        owner = lax.div(col, leaf_tiles)
        acc[(owner ^ place) * leaf_tiles + col - owner * leaf_tiles] += buf[k]

    for i in range(parts):
        started[i].wait()

        def one(j, carry):
            add(acc_a, i * chunk + 2 * j)
            add(acc_b, i * chunk + 2 * j + 1)
            return carry

        lax.fori_loop(0, chunk // 2, one, 0, unroll=4)
    for i, out in enumerate(outs):
        for t in range(leaf_tiles):
            out[t] = acc_a[i * leaf_tiles + t] + acc_b[i * leaf_tiles + t]


def merge(couple, cols, leaf_tiles):
    k_all, tile, _ = couple.shape
    rows = lax.axis_size("row")
    chunk = 16 if k_all % 16 == 0 else k_all
    acc = pltpu.VMEM((rows * leaf_tiles, tile, tile), F32)
    scratch = [pltpu.VMEM(couple.shape, F32), acc, acc]
    return pl.pallas_call(
        functools.partial(merge_body, leaf_tiles, chunk), name="merge",
        in_specs=[HB, HB],
        out_specs=[VM] * rows, out_shape=[pltpu.VMEM((leaf_tiles, tile, tile), F32)] * rows,
        compiler_params=room(scratch),
        scratch_shapes=scratch + [
            pltpu.SMEM(cols.shape, jnp.int32), pltpu.SemaphoreType.DMA((k_all // chunk + 1,))],
    )(*[pltpu.with_memory_space_constraint(v, pltpu.HBM) for v in (cols, couple)])


def partial_body(count, *refs):
    mats, msgs = refs[:count], refs[count:2 * count]
    own, other, mine, buf = refs[2 * count:]
    leaf_tiles, tile, _ = mats[0].shape
    half = tile // 2
    core = lax.axis_index("layer") % 2
    wide, thin = None, None
    for i in range(count):
        mine[i] = msgs[i][leaf_tiles * tile:, :]
        right_side = split(msgs[i][:leaf_tiles * tile, :], 1)
        row = jnp.concatenate([mats[i][t] for t in range(leaf_tiles)], axis=1)
        high = row.astype(jnp.bfloat16)
        low = (row - high.astype(F32)).astype(jnp.bfloat16)
        a = jnp.dot(high, right_side, preferred_element_type=F32)
        b = jnp.dot(low, right_side[:, :right_side.shape[1] // 2], preferred_element_type=F32)
        wide = a if wide is None else wide + a
        thin = b if thin is None else thin + b
    cols = thin.shape[1]
    total = wide[:, :cols] + (wide[:, cols:] + thin)
    up = pl.multiple_of(core * half, half)
    down = pl.multiple_of((1 - core) * half, half)
    buf[...] = total.T
    own[...] = buf[pl.ds(up, half), :]
    other[...] = buf[pl.ds(down, half), :]


def stack_body(*refs):
    at = 0
    for ref in refs[:-1]:
        if len(ref.shape) == len(refs[-1].shape):
            refs[-1][at:at + ref.shape[0]] = ref[...]
            at += ref.shape[0]
        else:
            refs[-1][at] = ref[...]
            at += 1


def factor_body(*refs):
    parts = refs[:-6]
    at, a, tt, s, a_buf, l_buf = refs[-6:]
    count, tile, _ = a_buf.shape
    share = tile // len(parts)
    layer = lax.axis_index("layer")
    place = lax.axis_index("row")
    for j, part in enumerate(parts):
        rows = pl.ds(pl.multiple_of((layer ^ j) * share, share), share)
        for i in range(count):
            a_buf[place ^ i, rows, :] = part[i, :share, :]
            l_buf[place ^ i, rows, :] = part[i, share:, :]
    for r in range(count):
        wide = split(a_buf[r], 1)
        a[r] = wide
        at[r] = split(a_buf[r].T, 1)
        if r > 0:
            tt[r] = split(dot(a_buf[r], l_buf[r]).T, 1)
        if r < count - 1:
            s[r] = split(spread(l_buf[r + 1], wide), 1)


def solve_body(steps, *refs):
    at, a, tt, s = refs[:4]
    right = refs[4:6]
    z, buf = refs[6:]
    count = buf.shape[0]
    place = lax.axis_index("row")
    for near in range(2):
        for p, k in enumerate(steps):
            buf[place ^ (2 * k + near)] = right[near][p]
    c = [spread(buf[r], at[r]) for r in range(count)]
    y = [c[0]]
    for r in range(1, count):
        y.append(c[r] - spread(y[-1], tt[r]))
    d = [spread(y[r], a[r]) for r in range(count)]
    behind = d[-1]
    z[count - 1] = behind
    for r in range(count - 2, -1, -1):
        behind = d[r] - spread(behind, s[r])
        z[r] = behind


def final_body(count, *refs):
    ready = fetch(refs[:2], refs[7 + count:])
    z_mine, z_theirs, x = refs[2:5]
    mats = refs[5:5 + count]
    leaf, anc = refs[5 + count:7 + count]
    zt = refs[-1]
    leaf_tiles, tile, _ = refs[0].shape
    half = tile // 2
    core = lax.axis_index("layer") % 2
    place = lax.axis_index("row")
    zt[:, pl.ds(pl.multiple_of(core * half, half), half), :] = z_mine[...]
    zt[:, pl.ds(pl.multiple_of((1 - core) * half, half), half), :] = z_theirs[...]
    anc[...] = zt[place].T
    cols = zt.shape[1]
    both, single = None, None
    for i, mat in enumerate(mats):
        left = split(zt[place ^ i], 0)
        row = jnp.concatenate([mat[t] for t in range(leaf_tiles)], axis=1)
        high = row.astype(jnp.bfloat16)
        low_part = (row - high.astype(F32)).astype(jnp.bfloat16)
        p = jnp.dot(left, high, preferred_element_type=F32)
        q = jnp.dot(left[:cols], low_part, preferred_element_type=F32)
        both = p if both is None else both + p
        single = q if single is None else single + q
    total = both[:cols] + (both[cols:] + single)
    inv, low = ready(0), ready(1)
    below = None
    for t in range(leaf_tiles - 1, -1, -1):
        rows = slice(t * tile, (t + 1) * tile)
        source = x[rows, :].T - total[:, rows]
        if below is not None:
            source = source - dot(below, low[t])
        below = dot(source, inv[t])
        leaf[rows, :] = below.T


def gather_far(msg, far, relayed):
    out = [msg]
    for k in range(1, far):
        low = k & -k if relayed else k
        out.append(pair_swap(out[k - low], "row", 2 * low))
    return out


def gather_row(msg, far):
    out = []
    for piece in gather_far(msg, far, True):
        out += [piece, pair_swap(piece, "row", 1)]
    return out


def gather_stacked(msg, far):
    straight = gather_far(msg, far, False)
    mine, = call(stack_body, [shape(far, *msg.shape)], (), straight, stay=True)
    return (mine, pair_swap(mine, "row", 1)), range(far)


def per_device(rhs_leaf, rhs_anc, leaf_inv, leaf_low, couple, tile_cols, anc_inv, anc_low):
    leaf_tiles, tile, _ = leaf_inv.shape
    cols = rhs_leaf.shape[1]
    half = cols // 2
    count = lax.axis_size("row")
    far = count // 2
    decks = lax.axis_size("layer") // 2
    base = leaf_tiles * tile
    share = tile // lax.axis_size("layer")

    msg, right = call(
        leaf_body, (shape(base + 2 * share, cols), shape(half, tile)),
        (rhs_leaf, leaf_inv, leaf_low, anc_inv, anc_low, rhs_anc),
        scratch=[pltpu.VMEM((cols, tile), F32)], stay=True,
    )
    msgs = gather_row(msg, far)
    mats = merge(couple, tile_cols, leaf_tiles)
    columns = [mats[0]] + [pair_swap(mats[i], "row", i) for i in range(1, count)]

    own, other, mine = call(
        functools.partial(partial_body, count),
        [shape(half, tile)] * 2 + [shape(count, 2 * share, tile)],
        (), (*mats, *msgs), [pltpu.VMEM((cols, tile), F32)], stay=True,
    )
    part = own + pair_swap(other, "layer", 1)
    total = part
    for k in range(1, decks):
        total = total + pair_swap(part, "layer", 2 * k)
    pieces, piece_steps = gather_stacked(right - total, far)

    parts = []
    for k in range(decks):
        part = pair_swap(mine, "layer", 2 * k) if k else mine
        parts += [part, pair_swap(part, "layer", 1)]
    factors = call(
        factor_body,
        [shape(count, tile, 2 * tile, dtype=jnp.bfloat16)] * 4, (), parts,
        [pltpu.VMEM((count, tile, tile), F32)] * 2, stay=True,
    )
    z_mine, = call(
        functools.partial(solve_body, piece_steps), [shape(count, half, tile)],
        (), (*factors, *pieces), [pltpu.VMEM((count, half, tile), F32)], stay=True,
    )
    z_theirs = pair_swap(z_mine, "layer", 1)
    leaf, anc_out = call(
        functools.partial(final_body, count),
        (shape(base, cols), shape(tile, cols)),
        (leaf_inv, leaf_low), (z_mine, z_theirs, msg, *columns),
        [pltpu.VMEM((count, cols, tile), F32)],
    )
    return leaf, anc_out


def solution(mesh):
    placed = (
        P(("layer", "row"), None),
        P("row", None),
        P(("layer", "row"), None, None),
        P(("layer", "row"), None, None),
        P(("layer", "row"), None, None),
        P(("layer", "row"), None),
        P("row", None, None),
        P("row", None, None),
    )

    return jax.shard_map(
        per_device,
        mesh=mesh,
        in_specs=placed,
        out_specs=(P(("layer", "row"), None), P("row", None)),
        check_vma=False,
    )
```

time: 89.9 us -> 85.3 us (0.949)
  the two profiles are of different devices: /device:TPU:9 before, /device:TPU:13 now
where the time goes in v1:
time: 85.3 us; the launch traced here: 85.2 us
  waiting for transfers between devices  39.4 us (46%)
  starting transfers between devices  33.4 us (39%)
  Pallas kernels  11.7 us (14%)
    ppermute x24, waiting for transfers between devices, pair_swap(): return lax.ppermute(value, axis, [(i, i ^ distance) for i in range(count)])  39.4 us
    ppermute x24, starting transfers between devices, pair_swap(): return lax.ppermute(value, axis, [(i, i ^ distance) for i in range(count)])  33.4 us
    pallas_call x6, Pallas kernels, call(): pl.pallas_call(body, out_shape=list(outs), compiler_params=room(scratch,...  7.99 us
    pallas_call x1, Pallas kernels, merge(): pl.pallas_call(functools.partial(merge_body, leaf_tiles, chunk), name='me...  3.7 us
  transfers between devices with their start and end apart: 24, of which 11 were waited for; matrix products, arithmetic and copies ran while one was open for 0% of the time, Pallas kernels for 8%

profile of v1, /device:TPU:13, one launch (start us, length us, event | category | flops | bytes accessed | tf_op | source)
XLA Modules:
  0.0 85.2 jit_solution(12756243082455891776)
XLA Ops:
  0.6 1.7 %shard_map.95 = (f32[320,128]{1,0:T(8,128)S(1)}, f32[64,128]{1,0:T(8,128)S(1)}) custom-call(f32[256,128]{1,0:T(8,128)} %refs_0_.2, f32[2,128,128]{2,1,0:T(8,128)} %refs_0_.3, f32[1,128,128]{2,1,0:T(8,128)} %refs_1_.3, f32[1,128,128]{2,1,0:T(8,128)} %refs_3_.1, f32[1,128,128]{2,1,0:T(8,128)} %refs_4_.1, f32[128,128]{1,0:T(8,128)} %refs_5_.1), custom_call_target="tpu_custom_call" | custom-call | tf_op jit(solution)/shard_map/pallas_call | solution.py:54
  2.3 2.4 %collective-permute-start.3 = (f32[320,128]{1,0:T(8,128)S(1)}, f32[320,128]{1,0:T(8,128)S(1)}, u32[]{:S(2)}, u32[]{:S(2)}) collective-permute-start(f32[320,128]{1,0:T(8,128)S(1)} %get-tuple-element.27.refs_8_.refs_4_), channel_id=1, source_target_pairs={{0,4},{1,5},{2,6},{3,7},{4,0},{5,1},{6,2},{7,3},{8,12},{9,13},{10,... | collective-permute-start | bytes 491528 | tf_op jit(solution)/shard_map/ppermute | solution.py:78
  4.9 7.1 %collective-permute-done.3.refs_12_ = f32[320,128]{1,0:T(8,128)S(1)} collective-permute-done((f32[320,128]{1,0:T(8,128)S(1)}, f32[320,128]{1,0:T(8,128)S(1)}, u32[]{:S(2)}, u32[]{:S(2)}) %collective-permute-start.3) | collective-permute-done | bytes 163872 | tf_op jit(solution)/shard_map/ppermute | solution.py:78
  12.1 1.2 %collective-permute-start = (f32[320,128]{1,0:T(8,128)S(1)}, f32[320,128]{1,0:T(8,128)S(1)}, u32[]{:S(2)}, u32[]{:S(2)}) collective-permute-start(f32[320,128]{1,0:T(8,128)S(1)} %get-tuple-element.27.refs_8_.refs_4_), channel_id=1, source_target_pairs={{0,1},{1,0},{2,3},{3,2},{4,5},{5,4},{6,7},{7,6},{8,9},{9,8},{10,11... | collective-permute-start | bytes 491528 | tf_op jit(solution)/shard_map/ppermute | solution.py:78
  13.6 1.2 %collective-permute-start.2 = (f32[320,128]{1,0:T(8,128)S(1)}, f32[320,128]{1,0:T(8,128)S(1)}, u32[]{:S(2)}, u32[]{:S(2)}) collective-permute-start(f32[320,128]{1,0:T(8,128)S(1)} %collective-permute-done.1.refs_10_), channel_id=1, source_target_pairs={{0,1},{1,0},{2,3},{3,2},{4,5},{5,4},{6,7},{7,6},{8,9},{9,8},{10,11... | collective-permute-start | bytes 491528 | tf_op jit(solution)/shard_map/ppermute | solution.py:78
  14.8 2.5 %collective-permute-done.5.refs_14_ = f32[320,128]{1,0:T(8,128)S(1)} collective-permute-done((f32[320,128]{1,0:T(8,128)S(1)}, f32[320,128]{1,0:T(8,128)S(1)}, u32[]{:S(2)}, u32[]{:S(2)}) %collective-permute-start.5) | collective-permute-done | bytes 163872 | tf_op jit(solution)/shard_map/ppermute | solution.py:78
  17.3 1.2 %collective-permute-start.6 = (f32[320,128]{1,0:T(8,128)S(1)}, f32[320,128]{1,0:T(8,128)S(1)}, u32[]{:S(2)}, u32[]{:S(2)}) collective-permute-start(f32[320,128]{1,0:T(8,128)S(1)} %collective-permute-done.5.refs_14_), channel_id=1, source_target_pairs={{0,1},{1,0},{2,3},{3,2},{4,5},{5,4},{6,7},{7,6},{8,9},{9,8},{10,11... | collective-permute-start | bytes 491528 | tf_op jit(solution)/shard_map/ppermute | solution.py:78
  18.5 3.7 %merge.1 = (f32[2,128,128]{2,1,0:T(8,128)S(1)}, f32[2,128,128]{2,1,0:T(8,128)S(1)}, f32[2,128,128]{2,1,0:T(8,128)S(1)}, f32[2,128,128]{2,1,0:T(8,128)S(1)}, f32[...) custom-call(s32[1,128]{1,0:T(1,128)} %cols_far.1, ...), custom_call_target="tpu_custom_call" | custom-call | tf_op jit(solution)/shard_map/merge/pallas_call | solution.py:148
  23.0 3.5 %collective-permute-done.6.refs_15_ = f32[320,128]{1,0:T(8,128)S(1)} collective-permute-done((f32[320,128]{1,0:T(8,128)S(1)}, f32[320,128]{1,0:T(8,128)S(1)}, u32[]{:S(2)}, u32[]{:S(2)}) %collective-permute-start.6) | collective-permute-done | bytes 163872 | tf_op jit(solution)/shard_map/ppermute | solution.py:78
  27.0 0.8 collective-permute-start.8
  27.8 2.8 %collective-permute-start.10 = (f32[64,128]{1,0:T(8,128)S(1)}, f32[64,128]{1,0:T(8,128)S(1)}, u32[]{:S(2)}, u32[]{:S(2)}) collective-permute-start(f32[64,128]{1,0:T(8,128)S(1)} %get-tuple-element.35), channel_id=1, source_target_pairs={{0,8},{8,0},{16,24},{24,16},{1,9},{9,1},{17,25},{25,17},{2,10},{10... | collective-permute-start | bytes 98312 | tf_op jit(solution)/shard_map/ppermute | solution.py:78
  30.6 0.9 %collective-permute-done.10 = f32[64,128]{1,0:T(8,128)S(1)} collective-permute-done((f32[64,128]{1,0:T(8,128)S(1)}, f32[64,128]{1,0:T(8,128)S(1)}, u32[]{:S(2)}, u32[]{:S(2)}) %collective-permute-start.10) | collective-permute-done | bytes 32800 | tf_op jit(solution)/shard_map/ppermute | solution.py:78
  31.4 1.0 %collective-permute-start.11 = (f32[64,128]{1,0:T(8,128)S(1)}, f32[64,128]{1,0:T(8,128)S(1)}, u32[]{:S(2)}, u32[]{:S(2)}) collective-permute-start(f32[64,128]{1,0:T(8,128)S(1)} %add.6), channel_id=1, source_target_pairs={{0,16},{8,24},{16,0},{24,8},{1,17},{9,25},{17,1},{25,9},{2,18},{10... | collective-permute-start | bytes 98312 | tf_op jit(solution)/shard_map/ppermute | solution.py:78
  33.1 3.5 %collective-permute-start.9 = (f32[8,64,128]{2,1,0:T(8,128)S(1)}, f32[8,64,128]{2,1,0:T(8,128)S(1)}, u32[]{:S(2)}, u32[]{:S(2)}) collective-permute-start(f32[8,64,128]{2,1,0:T(8,128)S(1)} %collective-permute-done.8.refs_2_), channel_id=1, source_target_pairs={{0,8},{8,0},{16,24},{24,16},{1,9},{9,1},{17,25},{25,17},{2,10},{10... | collective-permute-start | bytes 786440 | tf_op jit(solution)/shard_map/ppermute | solution.py:78
  36.6 2.2 %collective-permute-start.12 = (f32[64,128]{1,0:T(8,128)S(1)}, f32[64,128]{1,0:T(8,128)S(1)}, u32[]{:S(2)}, u32[]{:S(2)}) collective-permute-start(f32[64,128]{1,0:T(8,128)S(1)} %add_subtract_fusion.refs_0_), channel_id=1, source_target_pairs={{0,2},{1,3},{2,0},{3,1},{4,6},{5,7},{6,4},{7,5},{8,10},{9,11},{10,... | collective-permute-start | bytes 98312 | tf_op jit(solution)/shard_map/ppermute | solution.py:78
  38.8 3.1 %collective-permute-start.13 = (f32[64,128]{1,0:T(8,128)S(1)}, f32[64,128]{1,0:T(8,128)S(1)}, u32[]{:S(2)}, u32[]{:S(2)}) collective-permute-start(f32[64,128]{1,0:T(8,128)S(1)} %add_subtract_fusion.refs_0_), channel_id=1, source_target_pairs={{0,4},{1,5},{2,6},{3,7},{4,0},{5,1},{6,2},{7,3},{8,12},{9,13},{10,... | collective-permute-start | bytes 98312 | tf_op jit(solution)/shard_map/ppermute | solution.py:78
  41.9 1.6 %collective-permute-done.13.refs_2_ = f32[64,128]{1,0:T(8,128)S(1)} collective-permute-done((f32[64,128]{1,0:T(8,128)S(1)}, f32[64,128]{1,0:T(8,128)S(1)}, u32[]{:S(2)}, u32[]{:S(2)}) %collective-permute-start.13) | collective-permute-done | bytes 32800 | tf_op jit(solution)/shard_map/ppermute | solution.py:78
  43.5 1.2 %collective-permute-done.14.refs_3_ = f32[64,128]{1,0:T(8,128)S(1)} collective-permute-done((f32[64,128]{1,0:T(8,128)S(1)}, f32[64,128]{1,0:T(8,128)S(1)}, u32[]{:S(2)}, u32[]{:S(2)}) %collective-permute-start.14) | collective-permute-done | bytes 32800 | tf_op jit(solution)/shard_map/ppermute | solution.py:78
  44.7 1.3 %collective-permute-start.15 = (f32[4,64,128]{2,1,0:T(8,128)S(1)}, f32[4,64,128]{2,1,0:T(8,128)S(1)}, u32[]{:S(2)}, u32[]{:S(2)}) collective-permute-start(f32[4,64,128]{2,1,0:T(8,128)S(1)} %shard_map.98.refs_4_), channel_id=1, source_target_pairs={{0,1},{1,0},{2,3},{3,2},{4,5},{5,4},{6,7},{7,6},{8,9},{9,8},{10,11... | collective-permute-start | bytes 393224 | tf_op jit(solution)/shard_map/ppermute | solution.py:78
  46.2 2.1 %collective-permute-start.18 = (f32[2,128,128]{2,1,0:T(8,128)S(1)}, f32[2,128,128]{2,1,0:T(8,128)S(1)}, u32[]{:S(2)}, u32[]{:S(2)}) collective-permute-start(f32[2,128,128]{2,1,0:T(8,128)S(1)} %get-tuple-element.21.refs_2_), channel_id=1, source_target_pairs={{0,2},{1,3},{2,0},{3,1},{4,6},{5,7},{6,4},{7,5},{8,10},{9,11},{10,... | collective-permute-start | bytes 393224 | tf_op jit(solution)/shard_map/ppermute | solution.py:78
  48.3 0.9 %collective-permute-start.19 = (f32[2,128,128]{2,1,0:T(8,128)S(1)}, f32[2,128,128]{2,1,0:T(8,128)S(1)}, u32[]{:S(2)}, u32[]{:S(2)}) collective-permute-start(f32[2,128,128]{2,1,0:T(8,128)S(1)} %get-tuple-element.22.refs_3_), channel_id=1, source_target_pairs={{0,3},{1,2},{2,1},{3,0},{4,7},{5,6},{6,5},{7,4},{8,11},{9,10},{10,... | collective-permute-start | bytes 393224 | tf_op jit(solution)/shard_map/ppermute | solution.py:78
  49.2 0.8 shard_map.97
  50.0 2.3 %shard_map.99.refs_2_ = f32[8,64,128]{2,1,0:T(8,128)S(1)} custom-call(bf16[8,128,256]{2,1,0:T(8,128)(2,1)S(1)} %get-tuple-element.29.refs_0_, bf16[8,128,256]{2,1,0:T(8,128)(2,1)S(1)} %get-tuple-element.30.refs_1_, bf16[8,128,256]{2,1,0:T(8,128)(2,1)S(1)} %get-tuple-element.31.refs_2_, bf16[8,128,256]{2,1,0:T(8,128)(2,1)S(1)} %get-tuple-element.32.refs_3_, ...), custom_call_target="tpu_custom_call" | custom-call | tf_op jit(solution)/shard_map/pallas_call | solution.py:54
  52.2 3.0 %collective-permute-start.16 = (f32[8,64,128]{2,1,0:T(8,128)S(1)}, f32[8,64,128]{2,1,0:T(8,128)S(1)}, u32[]{:S(2)}, u32[]{:S(2)}) collective-permute-start(f32[8,64,128]{2,1,0:T(8,128)S(1)} %shard_map.99.refs_2_), channel_id=1, source_target_pairs={{0,8},{8,0},{16,24},{24,16},{1,9},{9,1},{17,25},{25,17},{2,10},{10... | collective-permute-start | bytes 786440 | tf_op jit(solution)/shard_map/ppermute | solution.py:78
  55.2 2.5 %collective-permute-start.20 = (f32[2,128,128]{2,1,0:T(8,128)S(1)}, f32[2,128,128]{2,1,0:T(8,128)S(1)}, u32[]{:S(2)}, u32[]{:S(2)}) collective-permute-start(f32[2,128,128]{2,1,0:T(8,128)S(1)} %get-tuple-element.23.refs_4_), channel_id=1, source_target_pairs={{0,4},{1,5},{2,6},{3,7},{4,0},{5,1},{6,2},{7,3},{8,12},{9,13},{10,... | collective-permute-start | bytes 393224 | tf_op jit(solution)/shard_map/ppermute | solution.py:78
  57.7 1.1 %collective-permute-start.21 = (f32[2,128,128]{2,1,0:T(8,128)S(1)}, f32[2,128,128]{2,1,0:T(8,128)S(1)}, u32[]{:S(2)}, u32[]{:S(2)}) collective-permute-start(f32[2,128,128]{2,1,0:T(8,128)S(1)} %get-tuple-element.24.refs_5_), channel_id=1, source_target_pairs={{0,5},{1,4},{2,7},{3,6},{4,1},{5,0},{6,3},{7,2},{8,13},{9,12},{10,... | collective-permute-start | bytes 393224 | tf_op jit(solution)/shard_map/ppermute | solution.py:78
  58.8 1.8 %collective-permute-start.22 = (f32[2,128,128]{2,1,0:T(8,128)S(1)}, f32[2,128,128]{2,1,0:T(8,128)S(1)}, u32[]{:S(2)}, u32[]{:S(2)}) collective-permute-start(f32[2,128,128]{2,1,0:T(8,128)S(1)} %get-tuple-element.25.refs_6_), channel_id=1, source_target_pairs={{0,6},{1,7},{2,4},{3,5},{4,2},{5,3},{6,0},{7,1},{8,14},{9,15},{10,... | collective-permute-start | bytes 393224 | tf_op jit(solution)/shard_map/ppermute | solution.py:78
  60.6 11.1 %collective-permute-done.20.refs_9_ = f32[2,128,128]{2,1,0:T(8,128)S(1)} collective-permute-done((f32[2,128,128]{2,1,0:T(8,128)S(1)}, f32[2,128,128]{2,1,0:T(8,128)S(1)}, u32[]{:S(2)}, u32[]{:S(2)}) %collective-permute-start.20) | collective-permute-done | bytes 131104 | tf_op jit(solution)/shard_map/ppermute | solution.py:78
  71.7 2.8 %collective-permute-done.21.refs_10_ = f32[2,128,128]{2,1,0:T(8,128)S(1)} collective-permute-done((f32[2,128,128]{2,1,0:T(8,128)S(1)}, f32[2,128,128]{2,1,0:T(8,128)S(1)}, u32[]{:S(2)}, u32[]{:S(2)}) %collective-permute-start.21) | collective-permute-done | bytes 131104 | tf_op jit(solution)/shard_map/ppermute | solution.py:78
  74.5 4.0 %collective-permute-done.22.refs_11_ = f32[2,128,128]{2,1,0:T(8,128)S(1)} collective-permute-done((f32[2,128,128]{2,1,0:T(8,128)S(1)}, f32[2,128,128]{2,1,0:T(8,128)S(1)}, u32[]{:S(2)}, u32[]{:S(2)}) %collective-permute-start.22) | collective-permute-done | bytes 131104 | tf_op jit(solution)/shard_map/ppermute | solution.py:78
  78.6 3.9 %collective-permute-done.23.refs_12_ = f32[2,128,128]{2,1,0:T(8,128)S(1)} collective-permute-done((f32[2,128,128]{2,1,0:T(8,128)S(1)}, f32[2,128,128]{2,1,0:T(8,128)S(1)}, u32[]{:S(2)}, u32[]{:S(2)}) %collective-permute-start.23) | collective-permute-done | bytes 131104 | tf_op jit(solution)/shard_map/ppermute | solution.py:78
  82.4 2.7 %shard_map.100 = (f32[256,128]{1,0:T(8,128)}, f32[128,128]{1,0:T(8,128)}) custom-call(f32[2,128,128]{2,1,0:T(8,128)} %refs_0_.3, f32[1,128,128]{2,1,0:T(8,128)} %refs_1_.3, f32[8,64,128]{2,1,0:T(8,128)S(1)} %shard_map.99.refs_2_, f32[8,64,128]{2,1,0:T(8,128)S(1)} %collective-permute-done.16.refs_3_, f32[320,128]{1,0:T(8,128)S(1)} %get-tuple-element.27.refs_8_.refs_4_, ...), custom_call_target="tpu_custom_call" | custom-call | tf_op jit(solution)/shard_map/pallas_call | solution.py:54
  (25 shorter events, 2.7 us)
Async XLA Ops:
  2.3 9.7 %collective-permute-start.3 = (f32[320,128]{1,0:T(8,128)S(1)}, f32[320,128]{1,0:T(8,128)S(1)}, u32[]{:S(2)}, u32[]{:S(2)}) collective-permute-start(f32[320,128]{1,0:T(8,128)S(1)} %get-tuple-element.27.refs_8_.refs_4_), channel_id=1, source_target_pairs={{0,4},{1,5},{2,6},{3,7},{4,0},{5,1},{6,2},{7,3},{8,12},{9,13},{10,... | collective-permute-start | bytes 491528 | tf_op jit(solution)/shard_map/ppermute | solution.py:78
  4.7 8.8 %collective-permute-start.1 = (f32[320,128]{1,0:T(8,128)S(1)}, f32[320,128]{1,0:T(8,128)S(1)}, u32[]{:S(2)}, u32[]{:S(2)}) collective-permute-start(f32[320,128]{1,0:T(8,128)S(1)} %get-tuple-element.27.refs_8_.refs_4_), channel_id=1, source_target_pairs={{0,2},{1,3},{2,0},{3,1},{4,6},{5,7},{6,4},{7,5},{8,10},{9,11},{10,... | collective-permute-start | bytes 491528 | tf_op jit(solution)/shard_map/ppermute | solution.py:78
  12.0 5.3 %collective-permute-start.5 = (f32[320,128]{1,0:T(8,128)S(1)}, f32[320,128]{1,0:T(8,128)S(1)}, u32[]{:S(2)}, u32[]{:S(2)}) collective-permute-start(f32[320,128]{1,0:T(8,128)S(1)} %collective-permute-done.3.refs_12_), channel_id=1, source_target_pairs={{0,2},{1,3},{2,0},{3,1},{4,6},{5,7},{6,4},{7,5},{8,10},{9,11},{10,... | collective-permute-start | bytes 491528 | tf_op jit(solution)/shard_map/ppermute | solution.py:78
  12.1 10.1 %collective-permute-start = (f32[320,128]{1,0:T(8,128)S(1)}, f32[320,128]{1,0:T(8,128)S(1)}, u32[]{:S(2)}, u32[]{:S(2)}) collective-permute-start(f32[320,128]{1,0:T(8,128)S(1)} %get-tuple-element.27.refs_8_.refs_4_), channel_id=1, source_target_pairs={{0,1},{1,0},{2,3},{3,2},{4,5},{5,4},{6,7},{7,6},{8,9},{9,8},{10,11... | collective-permute-start | bytes 491528 | tf_op jit(solution)/shard_map/ppermute | solution.py:78
  13.3 9.7 %collective-permute-start.4 = (f32[320,128]{1,0:T(8,128)S(1)}, f32[320,128]{1,0:T(8,128)S(1)}, u32[]{:S(2)}, u32[]{:S(2)}) collective-permute-start(f32[320,128]{1,0:T(8,128)S(1)} %collective-permute-done.3.refs_12_), channel_id=1, source_target_pairs={{0,1},{1,0},{2,3},{3,2},{4,5},{5,4},{6,7},{7,6},{8,9},{9,8},{10,11... | collective-permute-start | bytes 491528 | tf_op jit(solution)/shard_map/ppermute | solution.py:78
  13.6 9.4 %collective-permute-start.2 = (f32[320,128]{1,0:T(8,128)S(1)}, f32[320,128]{1,0:T(8,128)S(1)}, u32[]{:S(2)}, u32[]{:S(2)}) collective-permute-start(f32[320,128]{1,0:T(8,128)S(1)} %collective-permute-done.1.refs_10_), channel_id=1, source_target_pairs={{0,1},{1,0},{2,3},{3,2},{4,5},{5,4},{6,7},{7,6},{8,9},{9,8},{10,11... | collective-permute-start | bytes 491528 | tf_op jit(solution)/shard_map/ppermute | solution.py:78
  17.3 9.2 %collective-permute-start.6 = (f32[320,128]{1,0:T(8,128)S(1)}, f32[320,128]{1,0:T(8,128)S(1)}, u32[]{:S(2)}, u32[]{:S(2)}) collective-permute-start(f32[320,128]{1,0:T(8,128)S(1)} %collective-permute-done.5.refs_14_), channel_id=1, source_target_pairs={{0,1},{1,0},{2,3},{3,2},{4,5},{5,4},{6,7},{7,6},{8,9},{9,8},{10,11... | collective-permute-start | bytes 491528 | tf_op jit(solution)/shard_map/ppermute | solution.py:78
  27.0 6.1 %collective-permute-start.8 = (f32[8,64,128]{2,1,0:T(8,128)S(1)}, f32[8,64,128]{2,1,0:T(8,128)S(1)}, u32[]{:S(2)}, u32[]{:S(2)}) collective-permute-start(f32[8,64,128]{2,1,0:T(8,128)S(1)} %get-tuple-element.28.refs_0_), channel_id=1, source_target_pairs={{0,16},{8,24},{16,0},{24,8},{1,17},{9,25},{17,1},{25,9},{2,18},{10... | collective-permute-start | bytes 786440 | tf_op jit(solution)/shard_map/ppermute | solution.py:78
  27.8 3.6 %collective-permute-start.10 = (f32[64,128]{1,0:T(8,128)S(1)}, f32[64,128]{1,0:T(8,128)S(1)}, u32[]{:S(2)}, u32[]{:S(2)}) collective-permute-start(f32[64,128]{1,0:T(8,128)S(1)} %get-tuple-element.35), channel_id=1, source_target_pairs={{0,8},{8,0},{16,24},{24,16},{1,9},{9,1},{17,25},{25,17},{2,10},{10... | collective-permute-start | bytes 98312 | tf_op jit(solution)/shard_map/ppermute | solution.py:78
  31.4 5.1 %collective-permute-start.11 = (f32[64,128]{1,0:T(8,128)S(1)}, f32[64,128]{1,0:T(8,128)S(1)}, u32[]{:S(2)}, u32[]{:S(2)}) collective-permute-start(f32[64,128]{1,0:T(8,128)S(1)} %add.6), channel_id=1, source_target_pairs={{0,16},{8,24},{16,0},{24,8},{1,17},{9,25},{17,1},{25,9},{2,18},{10... | collective-permute-start | bytes 98312 | tf_op jit(solution)/shard_map/ppermute | solution.py:78
  32.4 15.8 %collective-permute-start.7 = (f32[8,64,128]{2,1,0:T(8,128)S(1)}, f32[8,64,128]{2,1,0:T(8,128)S(1)}, u32[]{:S(2)}, u32[]{:S(2)}) collective-permute-start(f32[8,64,128]{2,1,0:T(8,128)S(1)} %get-tuple-element.28.refs_0_), channel_id=1, source_target_pairs={{0,8},{8,0},{16,24},{24,16},{1,9},{9,1},{17,25},{25,17},{2,10},{10... | collective-permute-start | bytes 786440 | tf_op jit(solution)/shard_map/ppermute | solution.py:78
  33.1 16.1 %collective-permute-start.9 = (f32[8,64,128]{2,1,0:T(8,128)S(1)}, f32[8,64,128]{2,1,0:T(8,128)S(1)}, u32[]{:S(2)}, u32[]{:S(2)}) collective-permute-start(f32[8,64,128]{2,1,0:T(8,128)S(1)} %collective-permute-done.8.refs_2_), channel_id=1, source_target_pairs={{0,8},{8,0},{16,24},{24,16},{1,9},{9,1},{17,25},{25,17},{2,10},{10... | collective-permute-start | bytes 786440 | tf_op jit(solution)/shard_map/ppermute | solution.py:78
  36.6 5.3 %collective-permute-start.12 = (f32[64,128]{1,0:T(8,128)S(1)}, f32[64,128]{1,0:T(8,128)S(1)}, u32[]{:S(2)}, u32[]{:S(2)}) collective-permute-start(f32[64,128]{1,0:T(8,128)S(1)} %add_subtract_fusion.refs_0_), channel_id=1, source_target_pairs={{0,2},{1,3},{2,0},{3,1},{4,6},{5,7},{6,4},{7,5},{8,10},{9,11},{10,... | collective-permute-start | bytes 98312 | tf_op jit(solution)/shard_map/ppermute | solution.py:78
  38.8 4.7 %collective-permute-start.13 = (f32[64,128]{1,0:T(8,128)S(1)}, f32[64,128]{1,0:T(8,128)S(1)}, u32[]{:S(2)}, u32[]{:S(2)}) collective-permute-start(f32[64,128]{1,0:T(8,128)S(1)} %add_subtract_fusion.refs_0_), channel_id=1, source_target_pairs={{0,4},{1,5},{2,6},{3,7},{4,0},{5,1},{6,2},{7,3},{8,12},{9,13},{10,... | collective-permute-start | bytes 98312 | tf_op jit(solution)/shard_map/ppermute | solution.py:78
  41.9 2.8 %collective-permute-start.14 = (f32[64,128]{1,0:T(8,128)S(1)}, f32[64,128]{1,0:T(8,128)S(1)}, u32[]{:S(2)}, u32[]{:S(2)}) collective-permute-start(f32[64,128]{1,0:T(8,128)S(1)} %add_subtract_fusion.refs_0_), channel_id=1, source_target_pairs={{0,6},{1,7},{2,4},{3,5},{4,2},{5,3},{6,0},{7,1},{8,14},{9,15},{10,... | collective-permute-start | bytes 98312 | tf_op jit(solution)/shard_map/ppermute | solution.py:78
  44.7 5.3 %collective-permute-start.15 = (f32[4,64,128]{2,1,0:T(8,128)S(1)}, f32[4,64,128]{2,1,0:T(8,128)S(1)}, u32[]{:S(2)}, u32[]{:S(2)}) collective-permute-start(f32[4,64,128]{2,1,0:T(8,128)S(1)} %shard_map.98.refs_4_), channel_id=1, source_target_pairs={{0,1},{1,0},{2,3},{3,2},{4,5},{5,4},{6,7},{7,6},{8,9},{9,8},{10,11... | collective-permute-start | bytes 393224 | tf_op jit(solution)/shard_map/ppermute | solution.py:78
  45.9 11.8 %collective-permute-start.17 = (f32[2,128,128]{2,1,0:T(8,128)S(1)}, f32[2,128,128]{2,1,0:T(8,128)S(1)}, u32[]{:S(2)}, u32[]{:S(2)}) collective-permute-start(f32[2,128,128]{2,1,0:T(8,128)S(1)} %get-tuple-element.20.refs_1_), channel_id=1, source_target_pairs={{0,1},{1,0},{2,3},{3,2},{4,5},{5,4},{6,7},{7,6},{8,9},{9,8},{10,11... | collective-permute-start | bytes 393224 | tf_op jit(solution)/shard_map/ppermute | solution.py:78
  46.2 12.6 %collective-permute-start.18 = (f32[2,128,128]{2,1,0:T(8,128)S(1)}, f32[2,128,128]{2,1,0:T(8,128)S(1)}, u32[]{:S(2)}, u32[]{:S(2)}) collective-permute-start(f32[2,128,128]{2,1,0:T(8,128)S(1)} %get-tuple-element.21.refs_2_), channel_id=1, source_target_pairs={{0,2},{1,3},{2,0},{3,1},{4,6},{5,7},{6,4},{7,5},{8,10},{9,11},{10,... | collective-permute-start | bytes 393224 | tf_op jit(solution)/shard_map/ppermute | solution.py:78
  48.3 12.4 %collective-permute-start.19 = (f32[2,128,128]{2,1,0:T(8,128)S(1)}, f32[2,128,128]{2,1,0:T(8,128)S(1)}, u32[]{:S(2)}, u32[]{:S(2)}) collective-permute-start(f32[2,128,128]{2,1,0:T(8,128)S(1)} %get-tuple-element.22.refs_3_), channel_id=1, source_target_pairs={{0,3},{1,2},{2,1},{3,0},{4,7},{5,6},{6,5},{7,4},{8,11},{9,10},{10,... | collective-permute-start | bytes 393224 | tf_op jit(solution)/shard_map/ppermute | solution.py:78
  52.2 30.2 %collective-permute-start.16 = (f32[8,64,128]{2,1,0:T(8,128)S(1)}, f32[8,64,128]{2,1,0:T(8,128)S(1)}, u32[]{:S(2)}, u32[]{:S(2)}) collective-permute-start(f32[8,64,128]{2,1,0:T(8,128)S(1)} %shard_map.99.refs_2_), channel_id=1, source_target_pairs={{0,8},{8,0},{16,24},{24,16},{1,9},{9,1},{17,25},{25,17},{2,10},{10... | collective-permute-start | bytes 786440 | tf_op jit(solution)/shard_map/ppermute | solution.py:78
  55.2 16.6 %collective-permute-start.20 = (f32[2,128,128]{2,1,0:T(8,128)S(1)}, f32[2,128,128]{2,1,0:T(8,128)S(1)}, u32[]{:S(2)}, u32[]{:S(2)}) collective-permute-start(f32[2,128,128]{2,1,0:T(8,128)S(1)} %get-tuple-element.23.refs_4_), channel_id=1, source_target_pairs={{0,4},{1,5},{2,6},{3,7},{4,0},{5,1},{6,2},{7,3},{8,12},{9,13},{10,... | collective-permute-start | bytes 393224 | tf_op jit(solution)/shard_map/ppermute | solution.py:78
  57.7 16.8 %collective-permute-start.21 = (f32[2,128,128]{2,1,0:T(8,128)S(1)}, f32[2,128,128]{2,1,0:T(8,128)S(1)}, u32[]{:S(2)}, u32[]{:S(2)}) collective-permute-start(f32[2,128,128]{2,1,0:T(8,128)S(1)} %get-tuple-element.24.refs_5_), channel_id=1, source_target_pairs={{0,5},{1,4},{2,7},{3,6},{4,1},{5,0},{6,3},{7,2},{8,13},{9,12},{10,... | collective-permute-start | bytes 393224 | tf_op jit(solution)/shard_map/ppermute | solution.py:78
  58.8 19.8 %collective-permute-start.22 = (f32[2,128,128]{2,1,0:T(8,128)S(1)}, f32[2,128,128]{2,1,0:T(8,128)S(1)}, u32[]{:S(2)}, u32[]{:S(2)}) collective-permute-start(f32[2,128,128]{2,1,0:T(8,128)S(1)} %get-tuple-element.25.refs_6_), channel_id=1, source_target_pairs={{0,6},{1,7},{2,4},{3,5},{4,2},{5,3},{6,0},{7,1},{8,14},{9,15},{10,... | collective-permute-start | bytes 393224 | tf_op jit(solution)/shard_map/ppermute | solution.py:78
  60.6 21.8 %collective-permute-start.23 = (f32[2,128,128]{2,1,0:T(8,128)S(1)}, f32[2,128,128]{2,1,0:T(8,128)S(1)}, u32[]{:S(2)}, u32[]{:S(2)}) collective-permute-start(f32[2,128,128]{2,1,0:T(8,128)S(1)} %get-tuple-element.26.refs_7_), channel_id=1, source_target_pairs={{0,7},{1,6},{2,5},{3,4},{4,3},{5,2},{6,1},{7,0},{8,15},{9,14},{10,... | collective-permute-start | bytes 393224 | tf_op jit(solution)/shard_map/ppermute | solution.py:78
